TPU v7x, 512 devices: a whole 4x8x8 slice. The times are simulated.
512 devices in a mesh: expert: 64 (over y, x, core), hidden: 8 (over z).
Axes of the slice: x: 4, y: 8, z: 8, core: 2. Of those that a mesh axis runs over, the one named last changes fastest.
Arguments:
- tokens: bfloat16 [4096, 4096], P('expert', 'hidden'), may hold values from -6 to 6
- expert_ids: int32 [4096, 8], P('expert'), may hold values from 0 to 63, all different within a row; in each aligned block of 64 rows (0 to 63, 64 to 127, ...) at most 16 rows name the same one
- gate_weights: float32 [4096, 8], P('expert'), may hold values from 0.05 to 0.5
- gate_proj: bfloat16 [64, 1536, 4096], P('expert', 'hidden'), may hold values from -0.09375 to 0.09375
- up_proj: bfloat16 [64, 1536, 4096], P('expert', 'hidden'), may hold values from -0.09375 to 0.09375
- down_proj: bfloat16 [64, 1536, 4096], P('expert', None, 'hidden'), may hold values from -0.15625 to 0.15625
Outputs:
- moe_out: bfloat16 [4096, 4096], P('expert', 'hidden')
Inputs may be any that keep to these rules, and one draw needn't show every extreme that they name: `expert_ids`: each row names 8 different experts; in each aligned block of 64 rows no expert is named by more than 16 rows.
All inputs are finite; a program needn't handle non-finite values.
Results may differ from a plain program's by a relative error of at most 0.0057.
Values may be sent and summed in bfloat16 or wider, within the bound.
No kernel may reach another device: no remote copies, remote signals or barrier semaphores. Data moves between devices by JAX's collectives and lax.ppermute only.
A program may use at most 64 MiB of HBM per device.

v0:
```python
import jax
import jax.numpy as jnp
from jax import lax
from jax.sharding import PartitionSpec as P


def on_device(tokens, expert_ids, gate_weights, gate_proj, up_proj, down_proj):
    local_count = gate_proj.shape[0]
    experts_all = local_count * lax.axis_size("expert")
    tok_rows = tokens.shape[0]
    top_count = expert_ids.shape[1]
    capacity = 2 * tok_rows * top_count // experts_all
    flat_ids = expert_ids.reshape(-1)
    onehot = (flat_ids[:, None] == jnp.arange(experts_all, dtype=jnp.int32)[None, :]).astype(
        jnp.int32
    )
    slot_index = jnp.sum((jnp.cumsum(onehot, axis=0) - onehot) * onehot, axis=1)
    position = flat_ids * capacity + slot_index
    token_of = jnp.arange(tok_rows * top_count, dtype=jnp.int32) // top_count
    full_rows = lax.all_gather(tokens, "hidden", axis=1, tiled=True)
    packed = jnp.zeros((experts_all * capacity, full_rows.shape[1]), full_rows.dtype)
    packed = packed.at[position].set(full_rows[token_of])
    arrived = lax.all_to_all(
        packed.reshape(experts_all, capacity, full_rows.shape[1]),
        "expert",
        split_axis=0,
        concat_axis=1,
        tiled=True,
    )
    gate_sum = jnp.einsum("lrd,lfd->lfr", arrived, gate_proj, preferred_element_type=jnp.float32)
    up_sum = jnp.einsum("lrd,lfd->lfr", arrived, up_proj, preferred_element_type=jnp.float32)
    activation = (jax.nn.silu(gate_sum) * up_sum).astype(jnp.bfloat16)
    expert_out = jnp.einsum(
        "lfr,lfd->lrd",
        lax.all_gather(activation, "hidden", axis=1, tiled=True),
        down_proj,
        preferred_element_type=jnp.float32,
    ).astype(jnp.bfloat16)
    returned = lax.all_to_all(expert_out, "expert", split_axis=1, concat_axis=0, tiled=True)
    gathered = returned.reshape(experts_all * capacity, returned.shape[2])[position]
    gathered = gathered.reshape(tok_rows, top_count, returned.shape[2]).astype(jnp.float32)
    mixed = jnp.sum(gathered * gate_weights[:, :, None], axis=1)
    return mixed.astype(jnp.bfloat16)


def solution(mesh):
    in_specs = (
        P("expert", "hidden"),
        P("expert", None),
        P("expert", None),
        P("expert", "hidden", None),
        P("expert", "hidden", None),
        P("expert", None, "hidden"),
    )
    out_specs = P("expert", "hidden")
    return jax.shard_map(
        on_device, mesh=mesh, in_specs=in_specs, out_specs=out_specs, check_vma=False
    )
```

profile of v0, /device:TPU:1, one launch (start us, length us, event | category | flops | bytes accessed | tf_op | source)
XLA Modules:
  0.0 375.7 jit_solution(17025929349063810798)
XLA Ops:
  6.5 0.0 copy-start
  6.5 0.0 all-gather.3.cloned.1.call-start
  6.5 0.9 copy.20
  7.4 0.1 eq.29
  7.5 0.1 eq.25
  7.6 0.7 broadcast_multiply_fusion
  8.3 1.2 reduce-window.6
  9.5 0.2 slice_reduce_fusion
  9.8 0.1 copy.19
  9.9 0.1 mul.38
  10.0 27.1 %all_gather.6 = bf16[64,4096]{1,0:T(8,128)(2,1)S(1)} all-gather(bf16[64,512]{1,0:T(8,128)(2,1)} %param.6), channel_id=1, replica_groups=mesh['expert'=64,'hidden'=8] {'hidden'}, dimensions={1}, use_global_device_ids=true | all-gather | bytes 589824 | tf_op jit(solution)/shard_map/all_gather | solution.py:20
  37.1 0.1 fusion.29
  37.3 4.4 %gather_fusion = bf16[512,4096]{1,0:T(8,128)(2,1)} fusion(bf16[64,4096]{1,0:T(8,128)(2,1)S(1)} %all_gather.6, s32[1024]{0:T(1024)S(1)} %pad_clamp_fusion.1), kind=kCustom, calls=%fused_computation | custom fusion | bytes 8390656 | tf_op jit(solution)/shard_map/gather | solution.py:22
  41.6 12.4 %scatter_custom_fusion = bf16[1024,4096]{1,0:T(8,128)(2,1)} fusion(s32[512]{0:T(512)S(1)} %bitcast.75, bf16[512,4096]{1,0:T(8,128)(2,1)} %gather_fusion, bf16[]{:T(256)} %constant.26.clone.1), kind=kCustom, calls=%fused_computation.3 | custom fusion | bytes 8389120 | tf_op jit(solution)/shard_map/scatter | solution.py:22
  54.1 201.0 %all_to_all.8 = bf16[64,16,4096]{2,1,0:T(8,128)(2,1)S(1)} all-to-all(bf16[64,16,4096]{2,1,0:T(8,128)(2,1)} %bitcast.68), channel_id=1, replica_groups=mesh['expert'=64,'hidden'=8] {'expert'}, dimensions={0} | all-to-all | bytes 16777216 | tf_op jit(solution)/shard_map/all_to_all | solution.py:23
  255.0 2.9 fusion.14
  258.0 3.7 fusion.23
  261.7 0.0 all-gather.3.cloned.1.call-update
  261.7 43.4 %all-gather.3.cloned.1.call-done = bf16[1536,1024]{1,0:T(8,128)(2,1)} async-done(((bf16[192,1024]{1,0:T(8,128)(2,1)}), bf16[1536,1024]{1,0:T(8,128)(2,1)}) %all-gather.3.cloned.1.call-update) | async-done | bytes 3145744 | tf_op jit(solution)/shard_map/all_gather | solution.py:35
  305.1 3.7 fusion.11
  308.8 3.0 copy.31
  311.8 0.5 broadcast.125
  312.3 8.3 %reduce.2 = bf16[1024,512]{1,0:T(8,128)(2,1)S(1)} reduce(bf16[1024,1,512]{2,1,0:T(2,128)(2,1)} %bitcast.73, bf16[]{:T(256)} %broadcast.125), dimensions={1}, to_apply=%bitcast.67.reduce_sub_computation | reduce | bytes 2097154
  320.6 1.6 reshape.173
  322.2 10.3 %all-to-all-start.1 = ((bf16[64,2,4096]{2,1,0:T(2,128)(2,1)}), bf16[64,2,4096]{2,1,0:T(2,128)(2,1)S(1)}, u32[]{:S(2)}, u32[]{:S(2)}) async-start(bf16[64,2,4096]{2,1,0:T(2,128)(2,1)} %reshape.173), calls=%async_computation.1 | async-start | bytes 2097152 | tf_op jit(solution)/shard_map/all_to_all | solution.py:39
  332.5 0.0 copy-done.1
  332.5 0.1 copy.24
  332.6 27.9 %all-to-all-done.1 = bf16[64,2,4096]{2,1,0:T(2,128)(2,1)S(1)} async-done(((bf16[64,2,4096]{2,1,0:T(2,128)(2,1)}), bf16[64,2,4096]{2,1,0:T(2,128)(2,1)S(1)}, u32[]{:S(2)}, u32[]{:S(2)}) %all-to-all-start.1) | async-done | bytes 1048608 | tf_op jit(solution)/shard_map/all_to_all | solution.py:39
  360.5 3.5 reshape.174
  364.0 1.9 copy.30
  365.9 2.0 gather_fusion.1
  367.8 1.0 fusion.26
  (13 shorter events, 0.1 us)
Async XLA Ops:
  6.5 298.6 %copy-start = (bf16[1,1536,512]{2,1,0:T(8,128)(2,1)S(1)}, bf16[1,1536,512]{2,1,0:T(8,128)(2,1)}, u32[]{:S(2)}) copy-start(bf16[1,1536,512]{2,1,0:T(8,128)(2,1)} %param.11) | copy-start | bytes 4718596
  6.5 298.6 %all-gather.3.cloned.1.call-start = ((), (), s32[]{:S(2)}) async-start(), calls=%async_computation.2 | async-start | bytes 3538944 | tf_op jit(solution)/shard_map/all_gather | solution.py:35
  54.1 201.0 %copy-start.2 = (bf16[1,192,4096]{2,1,0:T(8,128)(2,1)S(1)}, bf16[1,192,4096]{2,1,0:T(8,128)(2,1)}, u32[]{:S(2)}) copy-start(bf16[1,192,4096]{2,1,0:T(8,128)(2,1)} %param.9) | copy-start | bytes 4718596
  255.0 2.9 copy-start.3
  311.8 20.7 %copy-start.1 = (f32[64,8]{0,1:T(8,128)S(1)}, f32[64,8]{0,1:T(8,128)}, u32[]{:S(2)}) copy-start(f32[64,8]{0,1:T(8,128)} %param.8) | copy-start | bytes 6148
  322.2 38.3 %all-to-all-start.1 = ((bf16[64,2,4096]{2,1,0:T(2,128)(2,1)}), bf16[64,2,4096]{2,1,0:T(2,128)(2,1)S(1)}, u32[]{:S(2)}, u32[]{:S(2)}) async-start(bf16[64,2,4096]{2,1,0:T(2,128)(2,1)} %reshape.173), calls=%async_computation.1 | async-start | bytes 2097152 | tf_op jit(solution)/shard_map/all_to_all | solution.py:39
Sparse Core Ops, SparseCore 0:
  261.8 43.2 all-gather.2
where the time goes:
time: 376 us
  blocking collectives  228 us (61%)
  waiting for transfers between devices  71.3 us (19%)
  local copies, waits for them, and re-layouts  30.8 us (8%)
  between operations  13.5 us (4%)
  other arithmetic  11.3 us (3%)
  starting transfers between devices  10.4 us (3%)
  matrix products  10.3 us (3%)
    all_to_all x1, blocking collectives, on_device(): lax.all_to_all(packed.reshape(experts_all, capacity, full_rows.shape[1]),...  201 us
    all_gather x1, waiting for transfers between devices, on_device(): lax.all_gather(activation, 'hidden', axis=1, tiled=True)  43.4 us
    all_to_all x1, waiting for transfers between devices, on_device(): lax.all_to_all(expert_out, 'expert', split_axis=1, concat_axis=0, tiled=T...  27.9 us
    all_gather x1, blocking collectives, on_device(): full_rows = lax.all_gather(tokens, 'hidden', axis=1, tiled=True)  27.1 us
    scatter x1, local copies, waits for them, and re-layouts, on_device(): packed = packed.at[position].set(full_rows[token_of])  12.4 us
    all_to_all x1, starting transfers between devices, on_device(): lax.all_to_all(expert_out, 'expert', split_axis=1, concat_axis=0, tiled=T...  10.3 us
    unnamed x14, local copies, waits for them, and re-layouts  8.43 us
    unnamed x1, other arithmetic  8.25 us
  transfers between devices with their start and end apart: 2, of which 2 were waited for; matrix products, arithmetic and copies ran while one was open for 0% of the time, Pallas kernels for 0%

commit v1 on v0

v1 whole, which is shorter than its diff:
```python
import functools

import jax
import jax.numpy as jnp
from jax import lax
from jax.experimental import pallas as pl
from jax.experimental.pallas import tpu as pltpu
from jax.sharding import PartitionSpec as P

BF16 = jnp.bfloat16
F32 = jnp.float32


def pack_kernel(ids_ref, tokens_ref, packed_ref, slots_ref):
    experts, tok_rows = slots_ref.shape
    lo, wide = packed_ref.shape[1:]
    width = tokens_ref.shape[1]
    expert = lax.broadcasted_iota(jnp.int32, (experts, tok_rows), 0)
    chosen = expert == ids_ref[0:1, :]
    for k in range(1, ids_ref.shape[0]):
        chosen = jnp.logical_or(chosen, expert == ids_ref[k : k + 1, :])
    before = lax.broadcasted_iota(jnp.int32, (tok_rows, tok_rows), 0)
    after = lax.broadcasted_iota(jnp.int32, (tok_rows, tok_rows), 1)
    earlier = jnp.where(before < after, 1.0, 0.0).astype(BF16)
    ranks = jnp.dot(jnp.where(chosen, 1.0, 0.0).astype(BF16), earlier, preferred_element_type=F32)
    slots = jnp.where(chosen, ranks, -1.0)
    slots_ref[...] = slots
    slot = lax.broadcasted_iota(jnp.int32, (experts, lo, tok_rows), 1).astype(F32)
    spread = jnp.broadcast_to(slots[:, None, :], (experts, lo, tok_rows))
    first = jnp.where(spread == slot, 1.0, 0.0).reshape(experts * lo, tok_rows).astype(BF16)
    rest = jnp.where(spread == slot + lo, 1.0, 0.0).reshape(experts * lo, tok_rows).astype(BF16)
    values = jnp.dot(first, tokens_ref[...], preferred_element_type=F32)
    packed_ref[:, :, :width] = values.reshape(experts, lo, width).astype(BF16)
    values = jnp.dot(rest, tokens_ref[:, : wide - width], preferred_element_type=F32)
    packed_ref[:, :, width:] = values.reshape(experts, lo, wide - width).astype(BF16)


def pack_rows(ids, tokens, experts, lo, near):
    tok_rows, width = tokens.shape
    return pl.pallas_call(
        pack_kernel,
        out_shape=(
            jax.ShapeDtypeStruct((experts, lo, width + near), BF16),
            jax.ShapeDtypeStruct((experts, tok_rows), F32),
        ),
        in_specs=[pl.BlockSpec(memory_space=pltpu.VMEM)] * 2,
        out_specs=[pl.BlockSpec(memory_space=pltpu.VMEM)] * 2,
        name="pack_rows",
    )(ids, tokens)


def hidden_kernel(lo, full_ref, weight_ref, far_ref, act_ref, total_ref):
    step = pl.program_id(0)
    per, rows, wide = full_ref.shape
    width, units = weight_ref.shape[1], weight_ref.shape[2] // 2
    near = wide - width
    first = rest = None
    for i in range(per):
        weight = weight_ref[i]
        more = jnp.dot(full_ref[i, :, :width], weight, preferred_element_type=F32)
        first = more if first is None else first + more
        more = jnp.dot(full_ref[i, :, width:], weight[:near], preferred_element_type=F32)
        rest = more if rest is None else rest + more

    @pl.when(step == 0)
    def _():
        total_ref[0] = first
        total_ref[1] = rest + far_ref[...]

    @pl.when(step > 0)
    def _():
        total_ref[0] += first
        total_ref[1] += rest

    @pl.when(step == pl.num_programs(0) - 1)
    def _():
        halves = [total_ref[group].reshape(rows // lo, lo, 2 * units) for group in range(2)]
        total = jnp.concatenate(halves, axis=1).reshape(2 * rows, 2 * units).T
        gate = total[:units]
        act_ref[...] = (gate / (1.0 + jnp.exp(-gate)) * total[units:]).astype(BF16)


def hidden_units(full, weight, far_sums, lo):
    n_hidden, rows, wide = full.shape
    width, pair = weight.shape[1:]
    per = 4
    return pl.pallas_call(
        functools.partial(hidden_kernel, lo),
        grid=(n_hidden // per,),
        out_shape=jax.ShapeDtypeStruct((pair // 2, rows * 2), BF16),
        in_specs=[
            pl.BlockSpec((per, rows, wide), lambda h: (h, 0, 0)),
            pl.BlockSpec((per, width, pair), lambda h: (h, 0, 0)),
            pl.BlockSpec((rows, pair), lambda h: (0, 0)),
        ],
        out_specs=pl.BlockSpec((pair // 2, rows * 2), lambda h: (0, 0)),
        scratch_shapes=[pltpu.VMEM((2, rows, pair), F32)],
        compiler_params=pltpu.CompilerParams(vmem_limit_bytes=56 << 20),
        name="hidden_units",
    )(full, weight, far_sums)


def on_device(tokens, expert_ids, gate_weights, gate_proj, up_proj, down_proj):
    n_hidden = lax.axis_size("hidden")
    here = lax.axis_index("hidden")
    experts_all = gate_proj.shape[0] * lax.axis_size("expert")
    tok_rows, width = tokens.shape
    top_count = expert_ids.shape[1]
    capacity = 2 * tok_rows * top_count // experts_all
    lo = capacity // 2
    near = width // 2
    rows = experts_all * lo

    def exchange(values):
        return lax.all_to_all(values, "expert", split_axis=0, concat_axis=0, tiled=True)

    packed, slots = pack_rows(expert_ids.T, tokens, experts_all, lo, near)
    packed, far = lax.optimization_barrier((packed, tokens[:, near:]))
    arrived = exchange(packed)
    reach = 1
    while reach < n_hidden:
        other = lax.ppermute(far, "hidden", [(i, i ^ reach) for i in range(n_hidden)])
        upper = (here & reach) != 0
        far = jnp.concatenate([jnp.where(upper, other, far), jnp.where(upper, far, other)], axis=1)
        reach *= 2
    picks = slots[:, None, :] == jnp.arange(capacity, dtype=F32)[None, :, None]
    packed_far = jnp.einsum(
        "est,td->esd", picks[:, lo:].astype(BF16), far, preferred_element_type=F32
    ).astype(BF16)
    arrived, packed_far = lax.optimization_barrier((arrived, packed_far))
    full = lax.all_gather(arrived.reshape(rows, width + near), "hidden", axis=0, tiled=False)
    arrived_far = exchange(packed_far).reshape(rows, n_hidden * (width - near))
    weight = jnp.concatenate([gate_proj[0], up_proj[0]], axis=0).T.reshape(n_hidden, width, -1)
    far_weight = weight[:, near:].reshape(n_hidden * (width - near), -1)
    far_sums = jnp.dot(arrived_far, far_weight, preferred_element_type=F32)
    activation = hidden_units(full, weight, far_sums, lo)
    expert_out = jnp.einsum(
        "fr,fd->rd",
        lax.all_gather(activation, "hidden", axis=0, tiled=True),
        down_proj[0],
        preferred_element_type=F32,
    ).astype(BF16)
    returned = exchange(expert_out.reshape(experts_all, capacity, width))
    hits = expert_ids[:, :, None] == jnp.arange(experts_all, dtype=jnp.int32)
    weights = jnp.sum(jnp.where(hits, gate_weights[:, :, None], 0.0), axis=1)
    combine = jnp.where(picks, weights.T[:, None, :], 0.0)
    mixed = jnp.einsum(
        "est,esd->td",
        combine,
        returned.astype(F32),
        precision=lax.Precision.HIGHEST,
        preferred_element_type=F32,
    )
    return mixed.astype(BF16)


def solution(mesh):
    in_specs = (
        P("expert", "hidden"),
        P("expert", None),
        P("expert", None),
        P("expert", "hidden", None),
        P("expert", "hidden", None),
        P("expert", None, "hidden"),
    )
    out_specs = P("expert", "hidden")
    return jax.shard_map(
        on_device, mesh=mesh, in_specs=in_specs, out_specs=out_specs, check_vma=False
    )
```

time: 376 us -> 241 us (0.64)
  blocking collectives: 228 us -> 0 us
  waiting for transfers between devices: 71.3 us -> 136 us
  starting transfers between devices: 10.4 us -> 55.1 us
  local copies, waits for them, and re-layouts: 30.8 us -> 8.4 us
  Pallas kernels: 0 us -> 10.8 us
  other arithmetic: 11.3 us -> 3.72 us
    all_to_all x1 -> x0, blocking collectives: 201 us -> none  [on_device(): lax.all_to_all(packed.reshape(experts_all, capacity, full_rows.shape[1]),...]
    all_to_all x1 -> x3, waiting for transfers between devices: 27.9 us -> 67.3 us  [exchange(): lax.all_to_all(values, 'expert', split_axis=0, concat_axis=0, tiled=True)]
    all_gather x1 -> x0, blocking collectives: 27.1 us -> none  [on_device(): full_rows = lax.all_gather(tokens, 'hidden', axis=1, tiled=True)]
    all_to_all x1 -> x3, starting transfers between devices: 10.3 us -> 36.8 us  [exchange(): lax.all_to_all(values, 'expert', split_axis=0, concat_axis=0, tiled=True)]
    all_gather x1 -> x2, waiting for transfers between devices: 43.4 us -> 63.2 us  [the longest x1 46.7 us: on_device(): lax.all_gather(activation, 'hidden', axis=0, tiled=True)]
    ppermute x0 -> x3, starting transfers between devices: none -> 18.3 us  [on_device(): lax.ppermute(far, 'hidden', [(i, i ^ reach) for i in range(n_hidden)])]
    scatter x1 -> x0, local copies, waits for them, and re-layouts: 12.4 us -> none  [on_device(): packed = packed.at[position].set(full_rows[token_of])]
    pallas_call x0 -> x2, Pallas kernels: none -> 10.8 us  [the longest x1 8.57 us: hidden_units(): pl.pallas_call(functools.partial(hidden_kernel, lo), grid=(n_hidden // pe...]
  transfers between devices with their start and end apart: 2 -> 8, of which waited for: 2 -> 7; matrix products, arithmetic and copies ran while one was open for 0% -> 7% of each run, Pallas kernels for 0% -> 0%
where the time goes in v1:
time: 241 us; the launch traced here: 240 us
  waiting for transfers between devices  136 us (56%)
  starting transfers between devices  55.1 us (23%)
  between operations  13.6 us (6%)
  matrix products  11.7 us (5%)
  Pallas kernels  10.8 us (4%)
  local copies, waits for them, and re-layouts  8.4 us (3%)
  other arithmetic  3.72 us (2%)
    all_to_all x3, waiting for transfers between devices, exchange(): lax.all_to_all(values, 'expert', split_axis=0, concat_axis=0, tiled=True)  67.3 us
    all_gather x1, waiting for transfers between devices, on_device(): lax.all_gather(activation, 'hidden', axis=0, tiled=True)  46.7 us
    all_to_all x3, starting transfers between devices, exchange(): lax.all_to_all(values, 'expert', split_axis=0, concat_axis=0, tiled=True)  36.8 us
    ppermute x3, starting transfers between devices, on_device(): lax.ppermute(far, 'hidden', [(i, i ^ reach) for i in range(n_hidden)])  18.3 us
    all_gather x1, waiting for transfers between devices, on_device(): lax.all_gather(arrived.reshape(rows, width + near), 'hidden', axis=0, til...  16.5 us
    pallas_call x1, Pallas kernels, hidden_units(): pl.pallas_call(functools.partial(hidden_kernel, lo), grid=(n_hidden // pe...  8.57 us
    ppermute x3, waiting for transfers between devices, on_device(): lax.ppermute(far, 'hidden', [(i, i ^ reach) for i in range(n_hidden)])  5.84 us
  transfers between devices with their start and end apart: 8, of which 7 were waited for; matrix products, arithmetic and copies ran while one was open for 7% of the time, Pallas kernels for 0%

profile of v1, /device:TPU:1, one launch (start us, length us, event | category | flops | bytes accessed | tf_op | source)
XLA Modules:
  0.0 239.7 jit_solution(3838360965269522877)
XLA Ops:
  6.5 0.9 slice.9
  7.4 2.3 pack_rows.1
  9.7 11.8 %all-to-all-start = ((bf16[64,8,768]{2,1,0:T(8,128)(2,1)}), bf16[64,8,768]{2,1,0:T(8,128)(2,1)S(1)}, u32[]{:S(2)}, u32[]{:S(2)}) async-start(bf16[64,8,768]{2,1,0:T(8,128)(2,1)} %get-tuple-element.13), calls=%async_computation | async-start | bytes 1572864 | tf_op jit(solution)/shard_map/all_to_all | solution.py:115
  21.4 0.0 all-gather.3.cloned.1.call-start
  21.5 4.0 %collective-permute-start = (bf16[64,256]{1,0:T(8,128)(2,1)S(1)}, bf16[64,256]{1,0:T(8,128)(2,1)S(1)}, u32[]{:S(2)}, u32[]{:S(2)}) collective-permute-start(bf16[64,256]{1,0:T(8,128)(2,1)S(1)} %slice.9), channel_id=1, source_target_pairs={{0,1},{1,0},{2,3},{3,2},{4,5},{5,4},{6,7},{7,6},{8,9},{9,8},{10,11... | collective-permute-start | bytes 98312 | tf_op jit(solution)/shard_map/ppermute | solution.py:122
  25.5 1.6 collective-permute-done
  27.1 5.8 %collective-permute-start.1 = (bf16[64,512]{1,0:T(8,128)(2,1)S(1)}, bf16[64,512]{1,0:T(8,128)(2,1)S(1)}, u32[]{:S(2)}, u32[]{:S(2)}) collective-permute-start(bf16[64,512]{1,0:T(8,128)(2,1)S(1)} %pad_maximum_fusion.1), channel_id=1, source_target_pairs={{0,2},{1,3},{2,0},{3,1},{4,6},{5,7},{6,4},{7,5},{8,10},{9,11},{10,... | collective-permute-start | bytes 196616 | tf_op jit(solution)/shard_map/ppermute | solution.py:122
  32.9 1.9 collective-permute-done.1
  34.9 8.4 %collective-permute-start.2 = (bf16[64,1024]{1,0:T(8,128)(2,1)S(1)}, bf16[64,1024]{1,0:T(8,128)(2,1)S(1)}, u32[]{:S(2)}, u32[]{:S(2)}) collective-permute-start(bf16[64,1024]{1,0:T(8,128)(2,1)S(1)} %pad_maximum_fusion), channel_id=1, source_target_pairs={{0,4},{1,5},{2,6},{3,7},{4,0},{5,1},{6,2},{7,3},{8,12},{9,13},{10,... | collective-permute-start | bytes 393224 | tf_op jit(solution)/shard_map/ppermute | solution.py:122
  43.4 0.1 iota_compare_fusion
  43.5 2.3 collective-permute-done.2
  45.9 2.0 convolution_convert_fusion
  47.9 0.9 copy-done.1
  48.8 0.0 all-gather.3.cloned.1.call-update
  48.8 14.5 %all-to-all-start.1 = ((bf16[64,8,2048]{2,1,0:T(8,128)(2,1)}), bf16[64,8,2048]{2,1,0:T(8,128)(2,1)}, u32[]{:S(2)}, u32[]{:S(2)}) async-start(bf16[64,8,2048]{2,1,0:T(8,128)(2,1)} %convolution_convert_fusion), calls=%async_computation.1 | async-start | bytes 4194304 | tf_op jit(solution)/shard_map/all_to_all | solution.py:115
  63.4 0.0 all-gather.5.cloned.1.call-start
  63.4 3.3 %maximum_bitcast_fusion = bf16[4096,384]{0,1:T(8,128)(2,1)} fusion(bf16[192,4096]{1,0:T(8,128)(2,1)S(1)} %bitcast.32, bf16[192,4096]{1,0:T(8,128)(2,1)} %bitcast.33), kind=kLoop, calls=%fused_computation | loop fusion | flops 6291456 | bytes 6291456 | tf_op jit(solution)/shard_map/transpose | solution.py:133
  66.7 4.8 %copy.20 = bf16[4096,384]{1,0:T(8,128)(2,1)} copy(bf16[4096,384]{0,1:T(8,128)(2,1)} %maximum_bitcast_fusion) | data formatting | bytes 6291456 | tf_op jit(solution)/shard_map/transpose | solution.py:133
  71.5 1.6 slice.13
  73.1 39.8 %all-to-all-done.1 = bf16[64,8,2048]{2,1,0:T(8,128)(2,1)} async-done(((bf16[64,8,2048]{2,1,0:T(8,128)(2,1)}), bf16[64,8,2048]{2,1,0:T(8,128)(2,1)}, u32[]{:S(2)}, u32[]{:S(2)}) %all-to-all-start.1) | async-done | bytes 2097184 | tf_op jit(solution)/shard_map/all_to_all | solution.py:115
  112.9 3.7 %fusion.far_ref = f32[512,384]{1,0:T(8,128)} fusion(bf16[2048,384]{1,0:T(8,128)(2,1)S(1)} %bitcast.31, bf16[64,8,2048]{2,1,0:T(8,128)(2,1)} %all-to-all-done.1), kind=kOutput, calls=%fused_computation.2 | convolution fusion | flops 805306368 | bytes 4456448 | tf_op jit(solution)/shard_map/dot_general | solution.py:135
  116.7 16.5 %all-gather.3.cloned.1.call-done.full_ref = bf16[8,512,768]{2,1,0:T(8,128)(2,1)} async-done(((bf16[1,512,768]{2,1,0:T(8,128)(2,1)}), bf16[8,512,768]{2,1,0:T(8,128)(2,1)}) %all-gather.3.cloned.1.call-update) | async-done | bytes 6291472 | tf_op jit(solution)/shard_map/all_gather | solution.py:131
  133.2 8.6 %hidden_units.1 = bf16[192,1024]{1,0:T(8,128)(2,1)} custom-call(bf16[8,512,768]{2,1,0:T(8,128)(2,1)} %all-gather.3.cloned.1.call-done.full_ref, bf16[8,512,384]{2,1,0:T(8,128)(2,1)} %bitcast.29, f32[512,384]{1,0:T(8,128)} %fusion.far_ref), custom_call_target="tpu_custom_call" | custom-call | tf_op jit(solution)/shard_map/hidden_units/pallas_call | solution.py:87
  141.8 46.7 %all-gather.5.cloned.1.call-done = bf16[1536,1024]{1,0:T(8,128)(2,1)} async-done(((bf16[192,1024]{1,0:T(8,128)(2,1)}), bf16[1536,1024]{1,0:T(8,128)(2,1)}) %all-gather.5.cloned.1.call-update) | async-done | bytes 3145744 | tf_op jit(solution)/shard_map/all_gather | solution.py:139
  188.5 4.7 %fusion.4 = bf16[1024,512]{1,0:T(8,128)(2,1)} fusion(bf16[1536,1024]{1,0:T(8,128)(2,1)} %all-gather.5.cloned.1.call-done, bf16[1,1536,512]{2,1,0:T(8,128)(2,1)S(1)} %copy-done), kind=kOutput, calls=%fused_computation.6 | convolution fusion | flops 1611137024 | bytes 5767168 | tf_op jit(solution)/shard_map/fr,fd->rd/dot_general | solution.py:137
  193.2 10.5 %all-to-all-start.2 = ((bf16[64,16,512]{2,1,0:T(8,128)(2,1)}), bf16[64,16,512]{2,1,0:T(8,128)(2,1)S(1)}, u32[]{:S(2)}, u32[]{:S(2)}) async-start(bf16[64,16,512]{2,1,0:T(8,128)(2,1)} %bitcast.34), calls=%async_computation.2 | async-start | bytes 2097152 | tf_op jit(solution)/shard_map/all_to_all | solution.py:115
  203.7 0.1 copy.17
  203.8 0.1 copy.18
  203.8 0.2 select_reduce_fusion
  204.1 0.1 copy.19
  204.1 27.5 %all-to-all-done.2 = bf16[64,16,512]{2,1,0:T(8,128)(2,1)S(1)} async-done(((bf16[64,16,512]{2,1,0:T(8,128)(2,1)}), bf16[64,16,512]{2,1,0:T(8,128)(2,1)S(1)}, u32[]{:S(2)}, u32[]{:S(2)}) %all-to-all-start.2) | async-done | bytes 1048608 | tf_op jit(solution)/shard_map/all_to_all | solution.py:115
  231.6 1.2 fusion.7
  (18 shorter events, 0.1 us)
Async XLA Ops:
  6.5 181.9 %copy-start = (bf16[1,1536,512]{2,1,0:T(8,128)(2,1)S(1)}, bf16[1,1536,512]{2,1,0:T(8,128)(2,1)}, u32[]{:S(2)}) copy-start(bf16[1,1536,512]{2,1,0:T(8,128)(2,1)} %param.11) | copy-start | bytes 4718596
  9.7 33.7 %copy-start.3 = (f32[64,64]{1,0:T(8,128)S(1)}, f32[64,64]{1,0:T(8,128)}, u32[]{:S(2)}) copy-start(f32[64,64]{1,0:T(8,128)} %get-tuple-element.11) | copy-start | bytes 49156
  9.7 38.2 %all-to-all-start = ((bf16[64,8,768]{2,1,0:T(8,128)(2,1)}), bf16[64,8,768]{2,1,0:T(8,128)(2,1)S(1)}, u32[]{:S(2)}, u32[]{:S(2)}) async-start(bf16[64,8,768]{2,1,0:T(8,128)(2,1)} %get-tuple-element.13), calls=%async_computation | async-start | bytes 1572864 | tf_op jit(solution)/shard_map/all_to_all | solution.py:115
  21.4 111.7 %all-gather.3.cloned.1.call-start = ((), (), s32[]{:S(2)}) async-start(), calls=%async_computation.3 | async-start | bytes 7077888 | tf_op jit(solution)/shard_map/all_gather | solution.py:131
  21.5 5.6 %collective-permute-start = (bf16[64,256]{1,0:T(8,128)(2,1)S(1)}, bf16[64,256]{1,0:T(8,128)(2,1)S(1)}, u32[]{:S(2)}, u32[]{:S(2)}) collective-permute-start(bf16[64,256]{1,0:T(8,128)(2,1)S(1)} %slice.9), channel_id=1, source_target_pairs={{0,1},{1,0},{2,3},{3,2},{4,5},{5,4},{6,7},{7,6},{8,9},{9,8},{10,11... | collective-permute-start | bytes 98312 | tf_op jit(solution)/shard_map/ppermute | solution.py:122
  27.1 7.8 %collective-permute-start.1 = (bf16[64,512]{1,0:T(8,128)(2,1)S(1)}, bf16[64,512]{1,0:T(8,128)(2,1)S(1)}, u32[]{:S(2)}, u32[]{:S(2)}) collective-permute-start(bf16[64,512]{1,0:T(8,128)(2,1)S(1)} %pad_maximum_fusion.1), channel_id=1, source_target_pairs={{0,2},{1,3},{2,0},{3,1},{4,6},{5,7},{6,4},{7,5},{8,10},{9,11},{10,... | collective-permute-start | bytes 196616 | tf_op jit(solution)/shard_map/ppermute | solution.py:122
  34.9 10.9 %collective-permute-start.2 = (bf16[64,1024]{1,0:T(8,128)(2,1)S(1)}, bf16[64,1024]{1,0:T(8,128)(2,1)S(1)}, u32[]{:S(2)}, u32[]{:S(2)}) collective-permute-start(bf16[64,1024]{1,0:T(8,128)(2,1)S(1)} %pad_maximum_fusion), channel_id=1, source_target_pairs={{0,4},{1,5},{2,6},{3,7},{4,0},{5,1},{6,2},{7,3},{8,12},{9,13},{10,... | collective-permute-start | bytes 393224 | tf_op jit(solution)/shard_map/ppermute | solution.py:122
  47.9 0.9 copy-start.1
  48.8 14.6 %copy-start.2 = (bf16[1,192,4096]{2,1,0:T(8,128)(2,1)S(1)}, bf16[1,192,4096]{2,1,0:T(8,128)(2,1)}, u32[]{:S(2)}) copy-start(bf16[1,192,4096]{2,1,0:T(8,128)(2,1)} %param.10) | copy-start | bytes 4718596
  48.8 64.1 %all-to-all-start.1 = ((bf16[64,8,2048]{2,1,0:T(8,128)(2,1)}), bf16[64,8,2048]{2,1,0:T(8,128)(2,1)}, u32[]{:S(2)}, u32[]{:S(2)}) async-start(bf16[64,8,2048]{2,1,0:T(8,128)(2,1)} %convolution_convert_fusion), calls=%async_computation.1 | async-start | bytes 4194304 | tf_op jit(solution)/shard_map/all_to_all | solution.py:115
  63.4 125.1 %all-gather.5.cloned.1.call-start = ((), (), s32[]{:S(2)}) async-start(), calls=%async_computation.4 | async-start | bytes 3538944 | tf_op jit(solution)/shard_map/all_gather | solution.py:139
  193.2 10.5 %copy-start.4 = (s32[64,8]{0,1:T(8,128)S(1)}, s32[64,8]{0,1:T(8,128)}, u32[]{:S(2)}) copy-start(s32[64,8]{0,1:T(8,128)} %param.7) | copy-start | bytes 6148
  193.2 10.6 %copy-start.5 = (f32[64,8]{0,1:T(8,128)S(1)}, f32[64,8]{0,1:T(8,128)}, u32[]{:S(2)}) copy-start(f32[64,8]{0,1:T(8,128)} %param.8) | copy-start | bytes 6148
  193.2 38.5 %all-to-all-start.2 = ((bf16[64,16,512]{2,1,0:T(8,128)(2,1)}), bf16[64,16,512]{2,1,0:T(8,128)(2,1)S(1)}, u32[]{:S(2)}, u32[]{:S(2)}) async-start(bf16[64,16,512]{2,1,0:T(8,128)(2,1)} %bitcast.34), calls=%async_computation.2 | async-start | bytes 2097152 | tf_op jit(solution)/shard_map/all_to_all | solution.py:115
Sparse Core Ops, SparseCore 0:
  48.9 84.2 all-gather.2
  141.9 46.5 all-gather.4

commit v2 on v0

v2 whole, which is shorter than its diff:
```python
import jax
import jax.numpy as jnp
from jax import lax
from jax.experimental import pallas as pl
from jax.experimental.pallas import tpu as pltpu
from jax.sharding import PartitionSpec as P

BF16 = jnp.bfloat16
F32 = jnp.float32


def pack_kernel(ids_ref, tokens_ref, first_ref, rest_ref, slots_ref):
    experts, tok_rows = slots_ref.shape
    lo = first_ref.shape[1]
    width = tokens_ref.shape[1]
    expert = lax.broadcasted_iota(jnp.int32, (experts, tok_rows), 0)
    chosen = expert == ids_ref[0:1, :]
    for k in range(1, ids_ref.shape[0]):
        chosen = jnp.logical_or(chosen, expert == ids_ref[k : k + 1, :])
    before = lax.broadcasted_iota(jnp.int32, (tok_rows, tok_rows), 0)
    after = lax.broadcasted_iota(jnp.int32, (tok_rows, tok_rows), 1)
    earlier = jnp.where(before < after, 1.0, 0.0).astype(BF16)
    ranks = jnp.dot(jnp.where(chosen, 1.0, 0.0).astype(BF16), earlier, preferred_element_type=F32)
    slots = jnp.where(chosen, ranks, -1.0)
    slots_ref[...] = slots
    slot = lax.broadcasted_iota(jnp.int32, (experts, lo, tok_rows), 1).astype(F32)
    spread = jnp.broadcast_to(slots[:, None, :], (experts, lo, tok_rows))
    for group, packed_ref in enumerate((first_ref, rest_ref)):
        picks = jnp.where(spread == slot + lo * group, 1.0, 0.0).reshape(experts * lo, tok_rows).astype(BF16)
        values = jnp.dot(picks, tokens_ref[...], preferred_element_type=F32)
        packed_ref[...] = values.reshape(experts, lo, width).astype(BF16)


def pack_rows(ids, tokens, experts, lo):
    tok_rows, width = tokens.shape
    packed = jax.ShapeDtypeStruct((experts, lo, width), BF16)
    return pl.pallas_call(
        pack_kernel,
        out_shape=(packed, packed, jax.ShapeDtypeStruct((experts, tok_rows), F32)),
        in_specs=[pl.BlockSpec(memory_space=pltpu.VMEM)] * 2,
        out_specs=[pl.BlockSpec(memory_space=pltpu.VMEM)] * 3,
        name="pack_rows",
    )(ids, tokens)


def on_device(tokens, expert_ids, gate_weights, gate_proj, up_proj, down_proj):
    n_hidden = lax.axis_size("hidden")
    here = lax.axis_index("hidden")
    experts_all = gate_proj.shape[0] * lax.axis_size("expert")
    tok_rows, width = tokens.shape
    units = gate_proj.shape[1]
    top_count = expert_ids.shape[1]
    capacity = 2 * tok_rows * top_count // experts_all
    lo = capacity // 2
    rows = experts_all * lo
    across = n_hidden // 2

    def exchange(values):
        return lax.all_to_all(values, "expert", split_axis=0, concat_axis=0, tiled=True)

    def fetch(values, ahead):
        return lax.ppermute(values, "hidden", [(i, (i - ahead) % n_hidden) for i in range(n_hidden)])

    def around(values):
        ahead = behind = values
        yield 0, values
        for step in range(1, across):
            behind, ahead = fetch(behind, -1), fetch(ahead, 1)
            yield n_hidden - step, behind
            yield step, ahead

    first, rest, slots = pack_rows(expert_ids.T, tokens, experts_all, lo)

    both = jnp.concatenate([gate_proj[0], up_proj[0]], axis=0)
    both = lax.dynamic_slice_in_dim(jnp.concatenate([both, both], axis=1), here * width, n_hidden * width, axis=1)
    down = lax.dynamic_slice_in_dim(
        jnp.concatenate([down_proj[0], down_proj[0]], axis=0), here * units, n_hidden * units, axis=0
    )
    first, own = lax.optimization_barrier((first, tokens))
    arrived = exchange(first)
    opposite = fetch(own, across)
    picks = slots[:, None, :] == jnp.arange(capacity, dtype=F32)[None, :, None]
    packed = jnp.concatenate(
        [
            jnp.einsum(
                "est,td->esd", picks[:, group * lo : (group + 1) * lo].astype(BF16), opposite, preferred_element_type=F32
            ).astype(BF16)
            for group in range(2)
        ],
        axis=2,
    )
    arrived, rest, both, down = lax.optimization_barrier((arrived, rest, both, down))
    arrived = [arrived, exchange(rest)]
    arrived[1], packed = lax.optimization_barrier((arrived[1], packed))
    opposite = exchange(packed).reshape(rows, 2 * width)

    activation = []
    for group in range(2):
        total = 0.0
        blocks = list(around(arrived[group].reshape(rows, width)))
        blocks.insert(-2, (across, opposite[:, group * width : (group + 1) * width]))
        for ahead, block in blocks:
            weight = both[:, ahead * width : (ahead + 1) * width]
            total = total + jnp.einsum("fd,rd->fr", weight, block, preferred_element_type=F32)
        activation.append((jax.nn.silu(total[:units]) * total[units:]).astype(BF16))
    activation = jnp.concatenate(activation, axis=1)

    hits = expert_ids[:, :, None] == jnp.arange(experts_all, dtype=jnp.int32)
    weights = jnp.sum(jnp.where(hits, gate_weights[:, :, None], 0.0), axis=1)
    combine = jnp.where(picks, weights.T[:, None, :], 0.0)

    def out_sums(block, ahead):
        return jnp.einsum("fr,fd->rd", block, down[ahead * units : (ahead + 1) * units], preferred_element_type=F32)

    blocks = list(around(activation))
    total = 0.0
    for ahead, block in blocks:
        total = total + out_sums(block, ahead)
    (_, behind), (_, ahead) = blocks[-2:]
    opposite = jnp.concatenate([fetch(behind[:, :rows], -1), fetch(ahead[:, rows:], 1)], axis=1)
    total = (total + out_sums(opposite, across)).astype(BF16)
    total = total.reshape(2, experts_all, lo, width).transpose(1, 0, 2, 3).reshape(experts_all, capacity, width)
    returned = exchange(total)
    mixed = jnp.einsum(
        "est,esd->td",
        combine,
        returned.astype(F32),
        precision=lax.Precision.HIGHEST,
        preferred_element_type=F32,
    )
    return mixed.astype(BF16)


def solution(mesh):
    in_specs = (
        P("expert", "hidden"),
        P("expert", None),
        P("expert", None),
        P("expert", "hidden", None),
        P("expert", "hidden", None),
        P("expert", None, "hidden"),
    )
    out_specs = P("expert", "hidden")
    return jax.shard_map(
        on_device, mesh=mesh, in_specs=in_specs, out_specs=out_specs, check_vma=False
    )
```

time: 376 us -> 248 us (0.66)
  blocking collectives: 228 us -> 0 us
  starting transfers between devices: 10.4 us -> 130 us
  local copies, waits for them, and re-layouts: 30.8 us -> 1.44 us
  matrix products: 10.3 us -> 31 us
  between operations: 13.5 us -> 0.61 us
    all_to_all x1 -> x0, blocking collectives: 201 us -> none  [on_device(): lax.all_to_all(packed.reshape(experts_all, capacity, full_rows.shape[1]),...]
    ppermute x0 -> x21, starting transfers between devices: none -> 78.8 us  [fetch(): lax.ppermute(values, 'hidden', [(i, (i - ahead) % n_hidden) for i in rang...]
    ppermute x0 -> x21, waiting for transfers between devices: none -> 44 us  [fetch(): lax.ppermute(values, 'hidden', [(i, (i - ahead) % n_hidden) for i in rang...]
    all_gather x1 -> x0, waiting for transfers between devices: 43.4 us -> none  [on_device(): lax.all_gather(activation, 'hidden', axis=1, tiled=True)]
    all_to_all x1 -> x4, starting transfers between devices: 10.3 us -> 51.6 us  [exchange(): lax.all_to_all(values, 'expert', split_axis=0, concat_axis=0, tiled=True)]
    all_gather x1 -> x0, blocking collectives: 27.1 us -> none  [on_device(): full_rows = lax.all_gather(tokens, 'hidden', axis=1, tiled=True)]
    dot_general x3 -> x27, matrix products: 10.3 us -> 31 us  [the longest x16 25 us: on_device(): jnp.einsum('fd,rd->fr', weight, block, preferred_element_type=F32)]
    scatter x1 -> x0, local copies, waits for them, and re-layouts: 12.4 us -> none  [on_device(): packed = packed.at[position].set(full_rows[token_of])]
  transfers between devices with their start and end apart: 2 -> 25, of which waited for: 2 -> 10; matrix products, arithmetic and copies ran while one was open for 0% -> 15% of each run, Pallas kernels for 0% -> 0%
where the time goes in v2:
time: 248 us; the launch traced here: 247 us
  starting transfers between devices  130 us (52%)
  waiting for transfers between devices  71.5 us (29%)
  matrix products  31 us (12%)
  other arithmetic  9.42 us (4%)
    ppermute x21, starting transfers between devices, fetch(): lax.ppermute(values, 'hidden', [(i, (i - ahead) % n_hidden) for i in rang...  78.8 us
    all_to_all x4, starting transfers between devices, exchange(): lax.all_to_all(values, 'expert', split_axis=0, concat_axis=0, tiled=True)  51.6 us
    ppermute x21, waiting for transfers between devices, fetch(): lax.ppermute(values, 'hidden', [(i, (i - ahead) % n_hidden) for i in rang...  44 us
    all_to_all x4, waiting for transfers between devices, exchange(): lax.all_to_all(values, 'expert', split_axis=0, concat_axis=0, tiled=True)  27.5 us
    dot_general x16, matrix products, on_device(): jnp.einsum('fd,rd->fr', weight, block, preferred_element_type=F32)  25 us
  transfers between devices with their start and end apart: 25, of which 10 were waited for; matrix products, arithmetic and copies ran while one was open for 15% of the time, Pallas kernels for 0%

profile of v2, /device:TPU:1, one launch (start us, length us, event | category | flops | bytes accessed | tf_op | source)
XLA Modules:
  0.0 246.7 jit_solution(1641105820596551545)
XLA Ops:
  0.0 2.2 pack_rows.1
  2.2 11.8 %all-to-all-start = ((bf16[64,8,512]{2,1,0:T(8,128)(2,1)}), bf16[64,8,512]{2,1,0:T(8,128)(2,1)}, u32[]{:S(2)}, u32[]{:S(2)}) async-start(bf16[64,8,512]{2,1,0:T(8,128)(2,1)} %get-tuple-element.18), calls=%async_computation | async-start | bytes 1048576 | tf_op jit(solution)/shard_map/all_to_all | solution.py:59
  14.1 10.6 %collective-permute-start.4 = (bf16[64,512]{1,0:T(8,128)(2,1)}, bf16[64,512]{1,0:T(8,128)(2,1)S(1)}, u32[]{:S(2)}, u32[]{:S(2)}) collective-permute-start(bf16[64,512]{1,0:T(8,128)(2,1)} %tokens_ref.1), channel_id=1, source_target_pairs={{0,4},{1,5},{2,6},{3,7},{4,0},{5,1},{6,2},{7,3},{8,12},{9,13},{10,... | collective-permute-start | bytes 196616 | tf_op jit(solution)/shard_map/ppermute | solution.py:62
  24.7 3.8 %fusion.3 = bf16[1536,512]{1,0:T(8,128)(2,1)} fusion(s32[]{:T(128)S(6)} %select_n.17, bf16[1536,512]{1,0:T(8,128)(2,1)} %bitcast.47), kind=kLoop, calls=%fused_computation.10 | loop fusion | flops 3145728 | bytes 3145732 | tf_op jit(solution)/shard_map/concatenate | solution.py:77
  28.5 4.0 %fusion.1 = bf16[384,4096]{1,0:T(8,128)(2,1)S(1)} fusion(s32[]{:T(128)S(6)} %select_n.16, bf16[192,4096]{1,0:T(8,128)(2,1)} %bitcast.48, bf16[192,4096]{1,0:T(8,128)(2,1)} %bitcast.49), kind=kLoop, calls=%fused_computation.5 | loop fusion | flops 12582912 | bytes 6291460 | tf_op jit(solution)/shard_map/concatenate | solution.py:75
  32.6 10.8 %all-to-all-start.1 = ((bf16[64,8,512]{2,1,0:T(8,128)(2,1)}), bf16[64,8,512]{2,1,0:T(8,128)(2,1)}, u32[]{:S(2)}, u32[]{:S(2)}) async-start(bf16[64,8,512]{2,1,0:T(8,128)(2,1)} %get-tuple-element.22), calls=%async_computation.1 | async-start | bytes 1048576 | tf_op jit(solution)/shard_map/all_to_all | solution.py:59
  43.7 3.0 %collective-permute-start = (bf16[512,512]{1,0:T(8,128)(2,1)}, bf16[512,512]{1,0:T(8,128)(2,1)}, u32[]{:S(2)}, u32[]{:S(2)}) collective-permute-start(bf16[512,512]{1,0:T(8,128)(2,1)} %bitcast.5), channel_id=1, source_target_pairs={{0,1},{1,2},{2,3},{3,4},{4,5},{5,6},{6,7},{7,0},{8,9},{9,10},{10,1... | collective-permute-start | bytes 1572872 | tf_op jit(solution)/shard_map/ppermute | solution.py:62
  46.7 3.8 %collective-permute-start.1 = (bf16[512,512]{1,0:T(8,128)(2,1)}, bf16[512,512]{1,0:T(8,128)(2,1)}, u32[]{:S(2)}, u32[]{:S(2)}) collective-permute-start(bf16[512,512]{1,0:T(8,128)(2,1)} %bitcast.5), channel_id=1, source_target_pairs={{0,7},{1,0},{2,1},{3,2},{4,3},{5,4},{6,5},{7,6},{8,15},{9,8},{10,9... | collective-permute-start | bytes 1572872 | tf_op jit(solution)/shard_map/ppermute | solution.py:62
  53.4 8.2 %collective-permute-done.1 = bf16[512,512]{1,0:T(8,128)(2,1)} collective-permute-done((bf16[512,512]{1,0:T(8,128)(2,1)}, bf16[512,512]{1,0:T(8,128)(2,1)}, u32[]{:S(2)}, u32[]{:S(2)}) %collective-permute-start.1) | collective-permute-done | bytes 524320 | tf_op jit(solution)/shard_map/ppermute | solution.py:62
  61.6 5.3 %collective-permute-start.3 = (bf16[512,512]{1,0:T(8,128)(2,1)}, bf16[512,512]{1,0:T(8,128)(2,1)}, u32[]{:S(2)}, u32[]{:S(2)}) collective-permute-start(bf16[512,512]{1,0:T(8,128)(2,1)} %collective-permute-done.1), channel_id=1, source_target_pairs={{0,7},{1,0},{2,1},{3,2},{4,3},{5,4},{6,5},{7,6},{8,15},{9,8},{10,9... | collective-permute-start | bytes 1572872 | tf_op jit(solution)/shard_map/ppermute | solution.py:62
  68.8 2.4 convolution_add_fusion.7
  71.2 11.8 %all-to-all-start.2 = ((bf16[64,8,1024]{2,1,0:T(8,128)(2,1)}), bf16[64,8,1024]{2,1,0:T(8,128)(2,1)}, u32[]{:S(2)}, u32[]{:S(2)}) async-start(bf16[64,8,1024]{2,1,0:T(8,128)(2,1)} %pad_maximum_fusion), calls=%async_computation.2 | async-start | bytes 2097152 | tf_op jit(solution)/shard_map/all_to_all | solution.py:59
  83.0 2.6 %convolution_add_fusion.6 = f32[384,512]{1,0:T(8,128)} fusion(f32[384,512]{1,0:T(8,128)} %convolution_add_fusion.7, bf16[512,512]{1,0:T(8,128)(2,1)} %collective-permute-done.1, bf16[384,4096]{1,0:T(8,128)(2,1)S(1)} %fusion.1), kind=kOutput, calls=%fused_computation.17 | convolution fusion | flops 201523200 | bytes 2490368 | tf_op jit(solution)/shard_map/fd,rd->fr/dot_general | solution.py:104
  87.6 4.9 %collective-permute-start.8 = (bf16[512,512]{1,0:T(8,128)(2,1)}, bf16[512,512]{1,0:T(8,128)(2,1)S(1)}, u32[]{:S(2)}, u32[]{:S(2)}) collective-permute-start(bf16[512,512]{1,0:T(8,128)(2,1)} %bitcast.8), channel_id=1, source_target_pairs={{0,7},{1,0},{2,1},{3,2},{4,3},{5,4},{6,5},{7,6},{8,15},{9,8},{10,9... | collective-permute-start | bytes 1572872 | tf_op jit(solution)/shard_map/ppermute | solution.py:62
  93.9 3.4 %collective-permute-start.6 = (bf16[512,512]{1,0:T(8,128)(2,1)}, bf16[512,512]{1,0:T(8,128)(2,1)S(1)}, u32[]{:S(2)}, u32[]{:S(2)}) collective-permute-start(bf16[512,512]{1,0:T(8,128)(2,1)} %collective-permute-done.3), channel_id=1, source_target_pairs={{0,7},{1,0},{2,1},{3,2},{4,3},{5,4},{6,5},{7,6},{8,15},{9,8},{10,9... | collective-permute-start | bytes 1572872 | tf_op jit(solution)/shard_map/ppermute | solution.py:62
  97.3 1.9 collective-permute-start.5
  99.2 2.3 fusion.32
  101.6 1.9 collective-permute-done.8
  103.5 5.3 %collective-permute-start.10 = (bf16[512,512]{1,0:T(8,128)(2,1)S(1)}, bf16[512,512]{1,0:T(8,128)(2,1)S(1)}, u32[]{:S(2)}, u32[]{:S(2)}) collective-permute-start(bf16[512,512]{1,0:T(8,128)(2,1)S(1)} %collective-permute-done.8), channel_id=1, source_target_pairs={{0,7},{1,0},{2,1},{3,2},{4,3},{5,4},{6,5},{7,6},{8,15},{9,8},{10,9... | collective-permute-start | bytes 1572872 | tf_op jit(solution)/shard_map/ppermute | solution.py:62
  112.5 13.4 %collective-permute-done.10 = bf16[512,512]{1,0:T(8,128)(2,1)S(1)} collective-permute-done((bf16[512,512]{1,0:T(8,128)(2,1)S(1)}, bf16[512,512]{1,0:T(8,128)(2,1)S(1)}, u32[]{:S(2)}, u32[]{:S(2)}) %collective-permute-start.10) | collective-permute-done | bytes 524320 | tf_op jit(solution)/shard_map/ppermute | solution.py:62
  125.9 5.3 %collective-permute-start.12 = (bf16[512,512]{1,0:T(8,128)(2,1)S(1)}, bf16[512,512]{1,0:T(8,128)(2,1)S(1)}, u32[]{:S(2)}, u32[]{:S(2)}) collective-permute-start(bf16[512,512]{1,0:T(8,128)(2,1)S(1)} %collective-permute-done.10), channel_id=1, source_target_pairs={{0,7},{1,0},{2,1},{3,2},{4,3},{5,4},{6,5},{7,6},{8,15},{9,8},{10,9... | collective-permute-start | bytes 1572872 | tf_op jit(solution)/shard_map/ppermute | solution.py:62
  132.5 2.1 collective-permute-start.11
  135.9 5.1 %collective-permute-done.12 = bf16[512,512]{1,0:T(8,128)(2,1)S(1)} collective-permute-done((bf16[512,512]{1,0:T(8,128)(2,1)S(1)}, bf16[512,512]{1,0:T(8,128)(2,1)S(1)}, u32[]{:S(2)}, u32[]{:S(2)}) %collective-permute-start.12) | collective-permute-done | bytes 524320 | tf_op jit(solution)/shard_map/ppermute | solution.py:62
  151.9 5.3 %collective-permute-start.14 = (bf16[192,1024]{1,0:T(8,128)(2,1)S(1)}, bf16[192,1024]{1,0:T(8,128)(2,1)S(1)}, u32[]{:S(2)}, u32[]{:S(2)}) collective-permute-start(bf16[192,1024]{1,0:T(8,128)(2,1)S(1)} %pad_maximum_fusion.1), channel_id=1, source_target_pairs={{0,7},{1,0},{2,1},{3,2},{4,3},{5,4},{6,5},{7,6},{8,15},{9,8},{10,9... | collective-permute-start | bytes 1179656 | tf_op jit(solution)/shard_map/ppermute | solution.py:62
  159.7 3.7 %collective-permute-done.14 = bf16[192,1024]{1,0:T(8,128)(2,1)S(1)} collective-permute-done((bf16[192,1024]{1,0:T(8,128)(2,1)S(1)}, bf16[192,1024]{1,0:T(8,128)(2,1)S(1)}, u32[]{:S(2)}, u32[]{:S(2)}) %collective-permute-start.14) | collective-permute-done | bytes 393248 | tf_op jit(solution)/shard_map/ppermute | solution.py:62
  163.3 5.3 %collective-permute-start.16 = (bf16[192,1024]{1,0:T(8,128)(2,1)S(1)}, bf16[192,1024]{1,0:T(8,128)(2,1)S(1)}, u32[]{:S(2)}, u32[]{:S(2)}) collective-permute-start(bf16[192,1024]{1,0:T(8,128)(2,1)S(1)} %collective-permute-done.14), channel_id=1, source_target_pairs={{0,7},{1,0},{2,1},{3,2},{4,3},{5,4},{6,5},{7,6},{8,15},{9,8},{10,9... | collective-permute-start | bytes 1179656 | tf_op jit(solution)/shard_map/ppermute | solution.py:62
  171.5 7.3 %collective-permute-done.15 = bf16[192,1024]{1,0:T(8,128)(2,1)S(1)} collective-permute-done((bf16[192,1024]{1,0:T(8,128)(2,1)S(1)}, bf16[192,1024]{1,0:T(8,128)(2,1)S(1)}, u32[]{:S(2)}, u32[]{:S(2)}) %collective-permute-start.15) | collective-permute-done | bytes 393248 | tf_op jit(solution)/shard_map/ppermute | solution.py:62
  180.8 4.6 %collective-permute-start.18 = (bf16[192,1024]{1,0:T(8,128)(2,1)S(1)}, bf16[192,1024]{1,0:T(8,128)(2,1)S(1)}, u32[]{:S(2)}, u32[]{:S(2)}) collective-permute-start(bf16[192,1024]{1,0:T(8,128)(2,1)S(1)} %collective-permute-done.16), channel_id=1, source_target_pairs={{0,7},{1,0},{2,1},{3,2},{4,3},{5,4},{6,5},{7,6},{8,15},{9,8},{10,9... | collective-permute-start | bytes 1179656 | tf_op jit(solution)/shard_map/ppermute | solution.py:62
  186.3 2.2 collective-permute-done.17
  190.6 4.6 %collective-permute-start.20 = (bf16[192,512]{1,0:T(8,128)(2,1)S(1)}, bf16[192,512]{1,0:T(8,128)(2,1)S(1)}, u32[]{:S(2)}, u32[]{:S(2)}) collective-permute-start(bf16[192,512]{1,0:T(8,128)(2,1)S(1)} %slice.121), channel_id=1, source_target_pairs={{0,7},{1,0},{2,1},{3,2},{4,3},{5,4},{6,5},{7,6},{8,15},{9,8},{10,9... | collective-permute-start | bytes 589832 | tf_op jit(solution)/shard_map/ppermute | solution.py:62
  200.2 17.2 %all-to-all-start.3 = ((bf16[64,16,512]{2,1,0:T(8,128)(2,1)}), bf16[64,16,512]{2,1,0:T(8,128)(2,1)S(1)}, u32[]{:S(2)}, u32[]{:S(2)}) async-start(bf16[64,16,512]{2,1,0:T(8,128)(2,1)} %bitcast.45), calls=%async_computation.3 | async-start | bytes 2097152 | tf_op jit(solution)/shard_map/all_to_all | solution.py:59
  217.9 27.5 %all-to-all-done.3 = bf16[64,16,512]{2,1,0:T(8,128)(2,1)S(1)} async-done(((bf16[64,16,512]{2,1,0:T(8,128)(2,1)}), bf16[64,16,512]{2,1,0:T(8,128)(2,1)S(1)}, u32[]{:S(2)}, u32[]{:S(2)}) %all-to-all-start.3) | async-done | bytes 1048608 | tf_op jit(solution)/shard_map/all_to_all | solution.py:59
  (80 shorter events, 42.3 us)
Async XLA Ops:
  2.2 30.3 %all-to-all-start = ((bf16[64,8,512]{2,1,0:T(8,128)(2,1)}), bf16[64,8,512]{2,1,0:T(8,128)(2,1)}, u32[]{:S(2)}, u32[]{:S(2)}) async-start(bf16[64,8,512]{2,1,0:T(8,128)(2,1)} %get-tuple-element.18), calls=%async_computation | async-start | bytes 1048576 | tf_op jit(solution)/shard_map/all_to_all | solution.py:59
  14.1 29.3 %collective-permute-start.4 = (bf16[64,512]{1,0:T(8,128)(2,1)}, bf16[64,512]{1,0:T(8,128)(2,1)S(1)}, u32[]{:S(2)}, u32[]{:S(2)}) collective-permute-start(bf16[64,512]{1,0:T(8,128)(2,1)} %tokens_ref.1), channel_id=1, source_target_pairs={{0,4},{1,5},{2,6},{3,7},{4,0},{5,1},{6,2},{7,3},{8,12},{9,13},{10,... | collective-permute-start | bytes 196616 | tf_op jit(solution)/shard_map/ppermute | solution.py:62
  28.5 4.0 %copy-start.7 = (f32[64,64]{1,0:T(8,128)S(1)}, f32[64,64]{1,0:T(8,128)}, u32[]{:S(2)}) copy-start(f32[64,64]{1,0:T(8,128)} %get-tuple-element.16) | copy-start | bytes 49156
  32.6 38.7 %all-to-all-start.1 = ((bf16[64,8,512]{2,1,0:T(8,128)(2,1)}), bf16[64,8,512]{2,1,0:T(8,128)(2,1)}, u32[]{:S(2)}, u32[]{:S(2)}) async-start(bf16[64,8,512]{2,1,0:T(8,128)(2,1)} %get-tuple-element.22), calls=%async_computation.1 | async-start | bytes 1048576 | tf_op jit(solution)/shard_map/all_to_all | solution.py:59
  43.7 23.2 %collective-permute-start = (bf16[512,512]{1,0:T(8,128)(2,1)}, bf16[512,512]{1,0:T(8,128)(2,1)}, u32[]{:S(2)}, u32[]{:S(2)}) collective-permute-start(bf16[512,512]{1,0:T(8,128)(2,1)} %bitcast.5), channel_id=1, source_target_pairs={{0,1},{1,2},{2,3},{3,4},{4,5},{5,6},{6,7},{7,0},{8,9},{9,10},{10,1... | collective-permute-start | bytes 1572872 | tf_op jit(solution)/shard_map/ppermute | solution.py:62
  46.7 14.9 %collective-permute-start.1 = (bf16[512,512]{1,0:T(8,128)(2,1)}, bf16[512,512]{1,0:T(8,128)(2,1)}, u32[]{:S(2)}, u32[]{:S(2)}) collective-permute-start(bf16[512,512]{1,0:T(8,128)(2,1)} %bitcast.5), channel_id=1, source_target_pairs={{0,7},{1,0},{2,1},{3,2},{4,3},{5,4},{6,5},{7,6},{8,15},{9,8},{10,9... | collective-permute-start | bytes 1572872 | tf_op jit(solution)/shard_map/ppermute | solution.py:62
  61.6 32.3 %collective-permute-start.3 = (bf16[512,512]{1,0:T(8,128)(2,1)}, bf16[512,512]{1,0:T(8,128)(2,1)}, u32[]{:S(2)}, u32[]{:S(2)}) collective-permute-start(bf16[512,512]{1,0:T(8,128)(2,1)} %collective-permute-done.1), channel_id=1, source_target_pairs={{0,7},{1,0},{2,1},{3,2},{4,3},{5,4},{6,5},{7,6},{8,15},{9,8},{10,9... | collective-permute-start | bytes 1572872 | tf_op jit(solution)/shard_map/ppermute | solution.py:62
  66.9 30.4 %collective-permute-start.2 = (bf16[512,512]{1,0:T(8,128)(2,1)}, bf16[512,512]{1,0:T(8,128)(2,1)}, u32[]{:S(2)}, u32[]{:S(2)}) collective-permute-start(bf16[512,512]{1,0:T(8,128)(2,1)} %collective-permute-done), channel_id=1, source_target_pairs={{0,1},{1,2},{2,3},{3,4},{4,5},{5,6},{6,7},{7,0},{8,9},{9,10},{10,1... | collective-permute-start | bytes 1572872 | tf_op jit(solution)/shard_map/ppermute | solution.py:62
  71.2 71.1 %all-to-all-start.2 = ((bf16[64,8,1024]{2,1,0:T(8,128)(2,1)}), bf16[64,8,1024]{2,1,0:T(8,128)(2,1)}, u32[]{:S(2)}, u32[]{:S(2)}) async-start(bf16[64,8,1024]{2,1,0:T(8,128)(2,1)} %pad_maximum_fusion), calls=%async_computation.2 | async-start | bytes 2097152 | tf_op jit(solution)/shard_map/all_to_all | solution.py:59
  85.7 23.1 %collective-permute-start.7 = (bf16[512,512]{1,0:T(8,128)(2,1)}, bf16[512,512]{1,0:T(8,128)(2,1)S(1)}, u32[]{:S(2)}, u32[]{:S(2)}) collective-permute-start(bf16[512,512]{1,0:T(8,128)(2,1)} %bitcast.8), channel_id=1, source_target_pairs={{0,1},{1,2},{2,3},{3,4},{4,5},{5,6},{6,7},{7,0},{8,9},{9,10},{10,1... | collective-permute-start | bytes 1572872 | tf_op jit(solution)/shard_map/ppermute | solution.py:62
  87.6 15.9 %collective-permute-start.8 = (bf16[512,512]{1,0:T(8,128)(2,1)}, bf16[512,512]{1,0:T(8,128)(2,1)S(1)}, u32[]{:S(2)}, u32[]{:S(2)}) collective-permute-start(bf16[512,512]{1,0:T(8,128)(2,1)} %bitcast.8), channel_id=1, source_target_pairs={{0,7},{1,0},{2,1},{3,2},{4,3},{5,4},{6,5},{7,6},{8,15},{9,8},{10,9... | collective-permute-start | bytes 1572872 | tf_op jit(solution)/shard_map/ppermute | solution.py:62
  93.9 37.3 %collective-permute-start.6 = (bf16[512,512]{1,0:T(8,128)(2,1)}, bf16[512,512]{1,0:T(8,128)(2,1)S(1)}, u32[]{:S(2)}, u32[]{:S(2)}) collective-permute-start(bf16[512,512]{1,0:T(8,128)(2,1)} %collective-permute-done.3), channel_id=1, source_target_pairs={{0,7},{1,0},{2,1},{3,2},{4,3},{5,4},{6,5},{7,6},{8,15},{9,8},{10,9... | collective-permute-start | bytes 1572872 | tf_op jit(solution)/shard_map/ppermute | solution.py:62
  97.3 49.6 %collective-permute-start.5 = (bf16[512,512]{1,0:T(8,128)(2,1)}, bf16[512,512]{1,0:T(8,128)(2,1)}, u32[]{:S(2)}, u32[]{:S(2)}) collective-permute-start(bf16[512,512]{1,0:T(8,128)(2,1)} %collective-permute-done.2), channel_id=1, source_target_pairs={{0,1},{1,2},{2,3},{3,4},{4,5},{5,6},{6,7},{7,0},{8,9},{9,10},{10,1... | collective-permute-start | bytes 1572872 | tf_op jit(solution)/shard_map/ppermute | solution.py:62
  103.5 22.4 %collective-permute-start.10 = (bf16[512,512]{1,0:T(8,128)(2,1)S(1)}, bf16[512,512]{1,0:T(8,128)(2,1)S(1)}, u32[]{:S(2)}, u32[]{:S(2)}) collective-permute-start(bf16[512,512]{1,0:T(8,128)(2,1)S(1)} %collective-permute-done.8), channel_id=1, source_target_pairs={{0,7},{1,0},{2,1},{3,2},{4,3},{5,4},{6,5},{7,6},{8,15},{9,8},{10,9... | collective-permute-start | bytes 1572872 | tf_op jit(solution)/shard_map/ppermute | solution.py:62
  108.8 23.7 %collective-permute-start.9 = (bf16[512,512]{1,0:T(8,128)(2,1)S(1)}, bf16[512,512]{1,0:T(8,128)(2,1)}, u32[]{:S(2)}, u32[]{:S(2)}) collective-permute-start(bf16[512,512]{1,0:T(8,128)(2,1)S(1)} %collective-permute-done.7), channel_id=1, source_target_pairs={{0,1},{1,2},{2,3},{3,4},{4,5},{5,6},{6,7},{7,0},{8,9},{9,10},{10,1... | collective-permute-start | bytes 1572872 | tf_op jit(solution)/shard_map/ppermute | solution.py:62
  125.9 15.1 %collective-permute-start.12 = (bf16[512,512]{1,0:T(8,128)(2,1)S(1)}, bf16[512,512]{1,0:T(8,128)(2,1)S(1)}, u32[]{:S(2)}, u32[]{:S(2)}) collective-permute-start(bf16[512,512]{1,0:T(8,128)(2,1)S(1)} %collective-permute-done.10), channel_id=1, source_target_pairs={{0,7},{1,0},{2,1},{3,2},{4,3},{5,4},{6,5},{7,6},{8,15},{9,8},{10,9... | collective-permute-start | bytes 1572872 | tf_op jit(solution)/shard_map/ppermute | solution.py:62
  132.5 17.7 %collective-permute-start.11 = (bf16[512,512]{1,0:T(8,128)(2,1)}, bf16[512,512]{1,0:T(8,128)(2,1)}, u32[]{:S(2)}, u32[]{:S(2)}) collective-permute-start(bf16[512,512]{1,0:T(8,128)(2,1)} %collective-permute-done.9), channel_id=1, source_target_pairs={{0,1},{1,2},{2,3},{3,4},{4,5},{5,6},{6,7},{7,0},{8,9},{9,10},{10,1... | collective-permute-start | bytes 1572872 | tf_op jit(solution)/shard_map/ppermute | solution.py:62
  142.3 3.0 %copy-start.1 = (f32[384,512]{1,0:T(8,128)S(1)}, f32[384,512]{1,0:T(8,128)}, u32[]{:S(2)}) copy-start(f32[384,512]{1,0:T(8,128)} %convolution_add_fusion.6) | copy-start | bytes 2359300
  142.3 3.0 %copy-start.5 = (f32[384,512]{1,0:T(8,128)S(1)}, f32[384,512]{1,0:T(8,128)}, u32[]{:S(2)}) copy-start(f32[384,512]{1,0:T(8,128)} %fusion.32) | copy-start | bytes 2359300
  146.9 1.7 copy-start.2
  150.2 9.0 %copy-start = (bf16[1536,512]{1,0:T(8,128)(2,1)S(1)}, bf16[1536,512]{1,0:T(8,128)(2,1)}, u32[]{:S(2)}) copy-start(bf16[1536,512]{1,0:T(8,128)(2,1)} %fusion.3) | copy-start | bytes 4718596
  151.9 11.4 %collective-permute-start.14 = (bf16[192,1024]{1,0:T(8,128)(2,1)S(1)}, bf16[192,1024]{1,0:T(8,128)(2,1)S(1)}, u32[]{:S(2)}, u32[]{:S(2)}) collective-permute-start(bf16[192,1024]{1,0:T(8,128)(2,1)S(1)} %pad_maximum_fusion.1), channel_id=1, source_target_pairs={{0,7},{1,0},{2,1},{3,2},{4,3},{5,4},{6,5},{7,6},{8,15},{9,8},{10,9... | collective-permute-start | bytes 1179656 | tf_op jit(solution)/shard_map/ppermute | solution.py:62
  157.3 11.4 %collective-permute-start.13 = (bf16[192,1024]{1,0:T(8,128)(2,1)S(1)}, bf16[192,1024]{1,0:T(8,128)(2,1)S(1)}, u32[]{:S(2)}, u32[]{:S(2)}) collective-permute-start(bf16[192,1024]{1,0:T(8,128)(2,1)S(1)} %pad_maximum_fusion.1), channel_id=1, source_target_pairs={{0,1},{1,2},{2,3},{3,4},{4,5},{5,6},{6,7},{7,0},{8,9},{9,10},{10,1... | collective-permute-start | bytes 1179656 | tf_op jit(solution)/shard_map/ppermute | solution.py:62
  163.3 17.4 %collective-permute-start.16 = (bf16[192,1024]{1,0:T(8,128)(2,1)S(1)}, bf16[192,1024]{1,0:T(8,128)(2,1)S(1)}, u32[]{:S(2)}, u32[]{:S(2)}) collective-permute-start(bf16[192,1024]{1,0:T(8,128)(2,1)S(1)} %collective-permute-done.14), channel_id=1, source_target_pairs={{0,7},{1,0},{2,1},{3,2},{4,3},{5,4},{6,5},{7,6},{8,15},{9,8},{10,9... | collective-permute-start | bytes 1179656 | tf_op jit(solution)/shard_map/ppermute | solution.py:62
  168.7 10.2 %collective-permute-start.15 = (bf16[192,1024]{1,0:T(8,128)(2,1)S(1)}, bf16[192,1024]{1,0:T(8,128)(2,1)S(1)}, u32[]{:S(2)}, u32[]{:S(2)}) collective-permute-start(bf16[192,1024]{1,0:T(8,128)(2,1)S(1)} %collective-permute-done.13), channel_id=1, source_target_pairs={{0,1},{1,2},{2,3},{3,4},{4,5},{5,6},{6,7},{7,0},{8,9},{9,10},{10,1... | collective-permute-start | bytes 1179656 | tf_op jit(solution)/shard_map/ppermute | solution.py:62
  178.9 9.7 %collective-permute-start.17 = (bf16[192,1024]{1,0:T(8,128)(2,1)S(1)}, bf16[192,1024]{1,0:T(8,128)(2,1)S(1)}, u32[]{:S(2)}, u32[]{:S(2)}) collective-permute-start(bf16[192,1024]{1,0:T(8,128)(2,1)S(1)} %collective-permute-done.15), channel_id=1, source_target_pairs={{0,1},{1,2},{2,3},{3,4},{4,5},{5,6},{6,7},{7,0},{8,9},{9,10},{10,1... | collective-permute-start | bytes 1179656 | tf_op jit(solution)/shard_map/ppermute | solution.py:62
  180.8 9.7 %collective-permute-start.18 = (bf16[192,1024]{1,0:T(8,128)(2,1)S(1)}, bf16[192,1024]{1,0:T(8,128)(2,1)S(1)}, u32[]{:S(2)}, u32[]{:S(2)}) collective-permute-start(bf16[192,1024]{1,0:T(8,128)(2,1)S(1)} %collective-permute-done.16), channel_id=1, source_target_pairs={{0,7},{1,0},{2,1},{3,2},{4,3},{5,4},{6,5},{7,6},{8,15},{9,8},{10,9... | collective-permute-start | bytes 1179656 | tf_op jit(solution)/shard_map/ppermute | solution.py:62
  188.6 7.6 %collective-permute-start.19 = (bf16[192,512]{1,0:T(8,128)(2,1)S(1)}, bf16[192,512]{1,0:T(8,128)(2,1)S(1)}, u32[]{:S(2)}, u32[]{:S(2)}) collective-permute-start(bf16[192,512]{1,0:T(8,128)(2,1)S(1)} %slice.120), channel_id=1, source_target_pairs={{0,1},{1,2},{2,3},{3,4},{4,5},{5,6},{6,7},{7,0},{8,9},{9,10},{10,1... | collective-permute-start | bytes 589832 | tf_op jit(solution)/shard_map/ppermute | solution.py:62
  190.6 7.2 %collective-permute-start.20 = (bf16[192,512]{1,0:T(8,128)(2,1)S(1)}, bf16[192,512]{1,0:T(8,128)(2,1)S(1)}, u32[]{:S(2)}, u32[]{:S(2)}) collective-permute-start(bf16[192,512]{1,0:T(8,128)(2,1)S(1)} %slice.121), channel_id=1, source_target_pairs={{0,7},{1,0},{2,1},{3,2},{4,3},{5,4},{6,5},{7,6},{8,15},{9,8},{10,9... | collective-permute-start | bytes 589832 | tf_op jit(solution)/shard_map/ppermute | solution.py:62
  199.1 18.4 %copy-start.8 = (s32[64,8]{0,1:T(8,128)S(1)}, s32[64,8]{0,1:T(8,128)}, u32[]{:S(2)}) copy-start(s32[64,8]{0,1:T(8,128)} %param.7) | copy-start | bytes 6148
  199.1 18.5 %copy-start.9 = (f32[64,8]{0,1:T(8,128)S(1)}, f32[64,8]{0,1:T(8,128)}, u32[]{:S(2)}) copy-start(f32[64,8]{0,1:T(8,128)} %param.8) | copy-start | bytes 6148
  200.2 45.2 %all-to-all-start.3 = ((bf16[64,16,512]{2,1,0:T(8,128)(2,1)}), bf16[64,16,512]{2,1,0:T(8,128)(2,1)S(1)}, u32[]{:S(2)}, u32[]{:S(2)}) async-start(bf16[64,16,512]{2,1,0:T(8,128)(2,1)} %bitcast.45), calls=%async_computation.3 | async-start | bytes 2097152 | tf_op jit(solution)/shard_map/all_to_all | solution.py:59
  (3 other events, 4.9 us)

commit v3 on v2

--- a/solution.py
+++ b/solution.py
@@ -53,7 +53,6 @@
     capacity = 2 * tok_rows * top_count // experts_all
     lo = capacity // 2
     rows = experts_all * lo
-    across = n_hidden // 2
 
     def exchange(values):
         return lax.all_to_all(values, "expert", split_axis=0, concat_axis=0, tiled=True)
@@ -61,13 +60,18 @@
     def fetch(values, ahead):
         return lax.ppermute(values, "hidden", [(i, (i - ahead) % n_hidden) for i in range(n_hidden)])
 
-    def around(values):
+    def around(values, group):
         ahead = behind = values
         yield 0, values
-        for step in range(1, across):
+        for step in range(1, n_hidden // 2):
             behind, ahead = fetch(behind, -1), fetch(ahead, 1)
             yield n_hidden - step, behind
             yield step, ahead
+        half = values.shape[0] // 2
+        if group == 0:
+            yield n_hidden // 2, fetch(behind, -1)
+        else:
+            yield n_hidden // 2, jnp.concatenate([fetch(behind[:half], -1), fetch(ahead[half:], 1)], axis=0)
 
     first, rest, slots = pack_rows(expert_ids.T, tokens, experts_all, lo)
 
@@ -76,47 +80,34 @@
     down = lax.dynamic_slice_in_dim(
         jnp.concatenate([down_proj[0], down_proj[0]], axis=0), here * units, n_hidden * units, axis=0
     )
-    first, own = lax.optimization_barrier((first, tokens))
     arrived = exchange(first)
-    opposite = fetch(own, across)
-    picks = slots[:, None, :] == jnp.arange(capacity, dtype=F32)[None, :, None]
-    packed = jnp.concatenate(
-        [
-            jnp.einsum(
-                "est,td->esd", picks[:, group * lo : (group + 1) * lo].astype(BF16), opposite, preferred_element_type=F32
-            ).astype(BF16)
-            for group in range(2)
-        ],
-        axis=2,
-    )
     arrived, rest, both, down = lax.optimization_barrier((arrived, rest, both, down))
     arrived = [arrived, exchange(rest)]
-    arrived[1], packed = lax.optimization_barrier((arrived[1], packed))
-    opposite = exchange(packed).reshape(rows, 2 * width)
 
     activation = []
     for group in range(2):
         total = 0.0
-        blocks = list(around(arrived[group].reshape(rows, width)))
-        blocks.insert(-2, (across, opposite[:, group * width : (group + 1) * width]))
-        for ahead, block in blocks:
+        for ahead, block in around(arrived[group].reshape(rows, width), group):
             weight = both[:, ahead * width : (ahead + 1) * width]
             total = total + jnp.einsum("fd,rd->fr", weight, block, preferred_element_type=F32)
         activation.append((jax.nn.silu(total[:units]) * total[units:]).astype(BF16))
     activation = jnp.concatenate(activation, axis=1)
 
+    picks = slots[:, None, :] == jnp.arange(capacity, dtype=F32)[None, :, None]
     hits = expert_ids[:, :, None] == jnp.arange(experts_all, dtype=jnp.int32)
     weights = jnp.sum(jnp.where(hits, gate_weights[:, :, None], 0.0), axis=1)
     combine = jnp.where(picks, weights.T[:, None, :], 0.0)
+    combine, activation = lax.optimization_barrier((combine, activation))
 
     def out_sums(block, ahead):
         return jnp.einsum("fr,fd->rd", block, down[ahead * units : (ahead + 1) * units], preferred_element_type=F32)
 
-    blocks = list(around(activation))
-    total = 0.0
-    for ahead, block in blocks:
-        total = total + out_sums(block, ahead)
-    (_, behind), (_, ahead) = blocks[-2:]
+    across = n_hidden // 2
+    total = out_sums(activation, 0)
+    ahead = behind = activation
+    for step in range(1, across):
+        behind, ahead = fetch(behind, -1), fetch(ahead, 1)
+        total = total + out_sums(behind, n_hidden - step) + out_sums(ahead, step)
     opposite = jnp.concatenate([fetch(behind[:, :rows], -1), fetch(ahead[:, rows:], 1)], axis=1)
     total = (total + out_sums(opposite, across)).astype(BF16)
     total = total.reshape(2, experts_all, lo, width).transpose(1, 0, 2, 3).reshape(experts_all, capacity, width)

time: 248 us -> 232 us (0.935)
  blocking collectives: 0 us -> 40.7 us
  starting transfers between devices: 130 us -> 100 us
  waiting for transfers between devices: 71.5 us -> 55.5 us
  matrix products: 31 us -> 20.1 us
    all_to_all x0 -> x1, blocking collectives: none -> 40.7 us  [exchange(): lax.all_to_all(values, 'expert', split_axis=0, concat_axis=0, tiled=True)]
    all_to_all x4 -> x2, starting transfers between devices: 51.6 us -> 18 us  [exchange(): lax.all_to_all(values, 'expert', split_axis=0, concat_axis=0, tiled=True)]
    all_to_all x4 -> x2, waiting for transfers between devices: 27.5 us -> 11.9 us  [exchange(): lax.all_to_all(values, 'expert', split_axis=0, concat_axis=0, tiled=True)]
    dot_general x16, matrix products: 25 us -> 13.6 us  [on_device(): jnp.einsum('fd,rd->fr', weight, block, preferred_element_type=F32)]
    ppermute x21 -> x23, starting transfers between devices: 78.8 us -> 82.3 us  [fetch(): lax.ppermute(values, 'hidden', [(i, (i - ahead) % n_hidden) for i in rang...]
    ppermute x21 -> x23, waiting for transfers between devices: 44 us -> 43.7 us  [fetch(): lax.ppermute(values, 'hidden', [(i, (i - ahead) % n_hidden) for i in rang...]
  transfers between devices with their start and end apart: 25 -> 25, of which waited for: 10 -> 14; matrix products, arithmetic and copies ran while one was open for 15% -> 11% of each run, Pallas kernels for 0% -> 0%
where the time goes in v3:
time: 232 us; the launch traced here: 230 us
  starting transfers between devices  100 us (43%)
  waiting for transfers between devices  55.5 us (24%)
  blocking collectives  40.7 us (18%)
  matrix products  20.1 us (9%)
  other arithmetic  9.07 us (4%)
    ppermute x23, starting transfers between devices, fetch(): lax.ppermute(values, 'hidden', [(i, (i - ahead) % n_hidden) for i in rang...  82.3 us
    ppermute x23, waiting for transfers between devices, fetch(): lax.ppermute(values, 'hidden', [(i, (i - ahead) % n_hidden) for i in rang...  43.7 us
    all_to_all x1, blocking collectives, exchange(): lax.all_to_all(values, 'expert', split_axis=0, concat_axis=0, tiled=True)  40.7 us
    all_to_all x2, starting transfers between devices, exchange(): lax.all_to_all(values, 'expert', split_axis=0, concat_axis=0, tiled=True)  18 us
    dot_general x16, matrix products, on_device(): jnp.einsum('fd,rd->fr', weight, block, preferred_element_type=F32)  13.6 us
    all_to_all x2, waiting for transfers between devices, exchange(): lax.all_to_all(values, 'expert', split_axis=0, concat_axis=0, tiled=True)  11.9 us
  transfers between devices with their start and end apart: 25, of which 14 were waited for; matrix products, arithmetic and copies ran while one was open for 11% of the time, Pallas kernels for 0%

profile of v3, /device:TPU:1, one launch (start us, length us, event | category | flops | bytes accessed | tf_op | source)
XLA Modules:
  0.0 230.5 jit_solution(157018948583133906)
XLA Ops:
  0.0 2.3 pack_rows.1
  2.3 11.8 %all-to-all-start = ((bf16[64,8,512]{2,1,0:T(8,128)(2,1)}), bf16[64,8,512]{2,1,0:T(8,128)(2,1)}, u32[]{:S(2)}, u32[]{:S(2)}) async-start(bf16[64,8,512]{2,1,0:T(8,128)(2,1)} %get-tuple-element.15), calls=%async_computation | async-start | bytes 1048576 | tf_op jit(solution)/shard_map/all_to_all | solution.py:58
  15.7 3.7 %fusion.3 = bf16[1536,512]{1,0:T(8,128)(2,1)} fusion(s32[]{:T(128)S(6)} %select_n.17, bf16[1536,512]{1,0:T(8,128)(2,1)} %bitcast.44), kind=kLoop, calls=%fused_computation.10 | loop fusion | flops 3145728 | bytes 3145732 | tf_op jit(solution)/shard_map/concatenate | solution.py:81
  19.4 4.0 %fusion.1 = bf16[384,4096]{1,0:T(8,128)(2,1)S(1)} fusion(s32[]{:T(128)S(6)} %select_n.16, bf16[192,4096]{1,0:T(8,128)(2,1)} %bitcast.45, bf16[192,4096]{1,0:T(8,128)(2,1)} %bitcast.46), kind=kLoop, calls=%fused_computation.5 | loop fusion | flops 12582912 | bytes 6291460 | tf_op jit(solution)/shard_map/concatenate | solution.py:79
  23.4 8.4 %all-to-all-done = bf16[64,8,512]{2,1,0:T(8,128)(2,1)} async-done(((bf16[64,8,512]{2,1,0:T(8,128)(2,1)}), bf16[64,8,512]{2,1,0:T(8,128)(2,1)}, u32[]{:S(2)}, u32[]{:S(2)}) %all-to-all-start) | async-done | bytes 524320 | tf_op jit(solution)/shard_map/all_to_all | solution.py:58
  31.8 4.0 %collective-permute-start = (bf16[512,512]{1,0:T(8,128)(2,1)}, bf16[512,512]{1,0:T(8,128)(2,1)}, u32[]{:S(2)}, u32[]{:S(2)}) collective-permute-start(bf16[512,512]{1,0:T(8,128)(2,1)} %bitcast.5), channel_id=1, source_target_pairs={{0,1},{1,2},{2,3},{3,4},{4,5},{5,6},{6,7},{7,0},{8,9},{9,10},{10,1... | collective-permute-start | bytes 1572872 | tf_op jit(solution)/shard_map/ppermute | solution.py:61
  35.7 8.6 %collective-permute-start.1 = (bf16[512,512]{1,0:T(8,128)(2,1)}, bf16[512,512]{1,0:T(8,128)(2,1)}, u32[]{:S(2)}, u32[]{:S(2)}) collective-permute-start(bf16[512,512]{1,0:T(8,128)(2,1)} %bitcast.5), channel_id=1, source_target_pairs={{0,7},{1,0},{2,1},{3,2},{4,3},{5,4},{6,5},{7,6},{8,15},{9,8},{10,9... | collective-permute-start | bytes 1572872 | tf_op jit(solution)/shard_map/ppermute | solution.py:61
  44.6 6.2 %all-to-all-start.1 = ((bf16[64,8,512]{2,1,0:T(8,128)(2,1)}), bf16[64,8,512]{2,1,0:T(8,128)(2,1)}, u32[]{:S(2)}, u32[]{:S(2)}) async-start(bf16[64,8,512]{2,1,0:T(8,128)(2,1)} %get-tuple-element.19), calls=%async_computation.1 | async-start | bytes 1048576 | tf_op jit(solution)/shard_map/all_to_all | solution.py:58
  56.6 4.6 %collective-permute-start.3 = (bf16[512,512]{1,0:T(8,128)(2,1)}, bf16[512,512]{1,0:T(8,128)(2,1)}, u32[]{:S(2)}, u32[]{:S(2)}) collective-permute-start(bf16[512,512]{1,0:T(8,128)(2,1)} %collective-permute-done.1), channel_id=1, source_target_pairs={{0,7},{1,0},{2,1},{3,2},{4,3},{5,4},{6,5},{7,6},{8,15},{9,8},{10,9... | collective-permute-start | bytes 1572872 | tf_op jit(solution)/shard_map/ppermute | solution.py:61
  62.6 2.3 %convolution_add_fusion.7 = f32[384,512]{1,0:T(8,128)} fusion(f32[384,512]{1,0:T(8,128)S(1)} %convolution_add_fusion.8, bf16[512,512]{1,0:T(8,128)(2,1)} %collective-permute-done.1, bf16[384,4096]{1,0:T(8,128)(2,1)S(1)} %fusion.1), kind=kOutput, calls=%fused_computation.18 | convolution fusion | flops 201523200 | bytes 2490368 | tf_op jit(solution)/shard_map/fd,rd->fr/dot_general | solution.py:92
  65.0 3.5 %all-to-all-done.1 = bf16[64,8,512]{2,1,0:T(8,128)(2,1)} async-done(((bf16[64,8,512]{2,1,0:T(8,128)(2,1)}), bf16[64,8,512]{2,1,0:T(8,128)(2,1)}, u32[]{:S(2)}, u32[]{:S(2)}) %all-to-all-start.1) | async-done | bytes 524320 | tf_op jit(solution)/shard_map/all_to_all | solution.py:58
  68.5 2.0 collective-permute-start.7
  70.5 4.6 %collective-permute-start.8 = (bf16[512,512]{1,0:T(8,128)(2,1)}, bf16[512,512]{1,0:T(8,128)(2,1)S(1)}, u32[]{:S(2)}, u32[]{:S(2)}) collective-permute-start(bf16[512,512]{1,0:T(8,128)(2,1)} %bitcast.6), channel_id=1, source_target_pairs={{0,7},{1,0},{2,1},{3,2},{4,3},{5,4},{6,5},{7,6},{8,15},{9,8},{10,9... | collective-permute-start | bytes 1572872 | tf_op jit(solution)/shard_map/ppermute | solution.py:61
  78.5 4.6 %collective-permute-start.5 = (bf16[512,512]{1,0:T(8,128)(2,1)}, bf16[512,512]{1,0:T(8,128)(2,1)S(1)}, u32[]{:S(2)}, u32[]{:S(2)}) collective-permute-start(bf16[512,512]{1,0:T(8,128)(2,1)} %collective-permute-done.3), channel_id=1, source_target_pairs={{0,7},{1,0},{2,1},{3,2},{4,3},{5,4},{6,5},{7,6},{8,15},{9,8},{10,9... | collective-permute-start | bytes 1572872 | tf_op jit(solution)/shard_map/ppermute | solution.py:61
  88.0 4.6 %collective-permute-start.10 = (bf16[512,512]{1,0:T(8,128)(2,1)S(1)}, bf16[512,512]{1,0:T(8,128)(2,1)S(1)}, u32[]{:S(2)}, u32[]{:S(2)}) collective-permute-start(bf16[512,512]{1,0:T(8,128)(2,1)S(1)} %collective-permute-done.8), channel_id=1, source_target_pairs={{0,7},{1,0},{2,1},{3,2},{4,3},{5,4},{6,5},{7,6},{8,15},{9,8},{10,9... | collective-permute-start | bytes 1572872 | tf_op jit(solution)/shard_map/ppermute | solution.py:61
  93.4 2.9 %collective-permute-done.4 = bf16[512,512]{1,0:T(8,128)(2,1)S(1)} collective-permute-done((bf16[512,512]{1,0:T(8,128)(2,1)}, bf16[512,512]{1,0:T(8,128)(2,1)S(1)}, u32[]{:S(2)}, u32[]{:S(2)}) %collective-permute-start.4) | collective-permute-done | bytes 524320 | tf_op jit(solution)/shard_map/ppermute | solution.py:61
  99.0 8.5 %collective-permute-done.9 = bf16[512,512]{1,0:T(8,128)(2,1)S(1)} collective-permute-done((bf16[512,512]{1,0:T(8,128)(2,1)S(1)}, bf16[512,512]{1,0:T(8,128)(2,1)S(1)}, u32[]{:S(2)}, u32[]{:S(2)}) %collective-permute-start.9) | collective-permute-done | bytes 524320 | tf_op jit(solution)/shard_map/ppermute | solution.py:61
  109.4 4.6 %collective-permute-start.12 = (bf16[512,512]{1,0:T(8,128)(2,1)S(1)}, bf16[512,512]{1,0:T(8,128)(2,1)S(1)}, u32[]{:S(2)}, u32[]{:S(2)}) collective-permute-start(bf16[512,512]{1,0:T(8,128)(2,1)S(1)} %collective-permute-done.10), channel_id=1, source_target_pairs={{0,7},{1,0},{2,1},{3,2},{4,3},{5,4},{6,5},{7,6},{8,15},{9,8},{10,9... | collective-permute-start | bytes 1572872 | tf_op jit(solution)/shard_map/ppermute | solution.py:61
  114.8 3.9 %collective-permute-done.6 = bf16[512,512]{1,0:T(8,128)(2,1)S(1)} collective-permute-done((bf16[512,512]{1,0:T(8,128)(2,1)S(1)}, bf16[512,512]{1,0:T(8,128)(2,1)S(1)}, u32[]{:S(2)}, u32[]{:S(2)}) %collective-permute-start.6) | collective-permute-done | bytes 524320 | tf_op jit(solution)/shard_map/ppermute | solution.py:61
  119.3 10.7 %collective-permute-done.11 = bf16[512,512]{1,0:T(8,128)(2,1)S(1)} collective-permute-done((bf16[512,512]{1,0:T(8,128)(2,1)S(1)}, bf16[512,512]{1,0:T(8,128)(2,1)S(1)}, u32[]{:S(2)}, u32[]{:S(2)}) %collective-permute-start.11) | collective-permute-done | bytes 524320 | tf_op jit(solution)/shard_map/ppermute | solution.py:61
  132.0 4.6 %collective-permute-start.14 = (bf16[256,512]{1,0:T(8,128)(2,1)S(1)}, bf16[256,512]{1,0:T(8,128)(2,1)S(1)}, u32[]{:S(2)}, u32[]{:S(2)}) collective-permute-start(bf16[256,512]{1,0:T(8,128)(2,1)S(1)} %slice.107), channel_id=1, source_target_pairs={{0,7},{1,0},{2,1},{3,2},{4,3},{5,4},{6,5},{7,6},{8,15},{9,8},{10,9... | collective-permute-start | bytes 786440 | tf_op jit(solution)/shard_map/ppermute | solution.py:61
  136.9 2.7 %collective-permute-done.13 = bf16[256,512]{1,0:T(8,128)(2,1)S(1)} collective-permute-done((bf16[256,512]{1,0:T(8,128)(2,1)S(1)}, bf16[256,512]{1,0:T(8,128)(2,1)S(1)}, u32[]{:S(2)}, u32[]{:S(2)}) %collective-permute-start.13) | collective-permute-done | bytes 262176 | tf_op jit(solution)/shard_map/ppermute | solution.py:61
  141.6 5.3 %collective-permute-start.16 = (bf16[192,1024]{1,0:T(8,128)(2,1)S(1)}, bf16[192,1024]{1,0:T(8,128)(2,1)S(1)}, u32[]{:S(2)}, u32[]{:S(2)}) collective-permute-start(bf16[192,1024]{1,0:T(8,128)(2,1)S(1)} %pad_maximum_fusion), channel_id=1, source_target_pairs={{0,7},{1,0},{2,1},{3,2},{4,3},{5,4},{6,5},{7,6},{8,15},{9,8},{10,9... | collective-permute-start | bytes 1179656 | tf_op jit(solution)/shard_map/ppermute | solution.py:61
  146.9 2.1 collective-permute-start.15
  149.5 3.3 %collective-permute-done.16 = bf16[192,1024]{1,0:T(8,128)(2,1)S(1)} collective-permute-done((bf16[192,1024]{1,0:T(8,128)(2,1)S(1)}, bf16[192,1024]{1,0:T(8,128)(2,1)S(1)}, u32[]{:S(2)}, u32[]{:S(2)}) %collective-permute-start.16) | collective-permute-done | bytes 393248 | tf_op jit(solution)/shard_map/ppermute | solution.py:61
  152.9 5.3 %collective-permute-start.18 = (bf16[192,1024]{1,0:T(8,128)(2,1)S(1)}, bf16[192,1024]{1,0:T(8,128)(2,1)S(1)}, u32[]{:S(2)}, u32[]{:S(2)}) collective-permute-start(bf16[192,1024]{1,0:T(8,128)(2,1)S(1)} %collective-permute-done.16), channel_id=1, source_target_pairs={{0,7},{1,0},{2,1},{3,2},{4,3},{5,4},{6,5},{7,6},{8,15},{9,8},{10,9... | collective-permute-start | bytes 1179656 | tf_op jit(solution)/shard_map/ppermute | solution.py:61
  161.1 2.1 collective-permute-done.18
  163.2 5.3 %collective-permute-start.20 = (bf16[192,1024]{1,0:T(8,128)(2,1)S(1)}, bf16[192,1024]{1,0:T(8,128)(2,1)S(1)}, u32[]{:S(2)}, u32[]{:S(2)}) collective-permute-start(bf16[192,1024]{1,0:T(8,128)(2,1)S(1)} %collective-permute-done.18), channel_id=1, source_target_pairs={{0,7},{1,0},{2,1},{3,2},{4,3},{5,4},{6,5},{7,6},{8,15},{9,8},{10,9... | collective-permute-start | bytes 1179656 | tf_op jit(solution)/shard_map/ppermute | solution.py:61
  173.3 5.0 %collective-permute-start.22 = (bf16[192,512]{1,0:T(8,128)(2,1)S(1)}, bf16[192,512]{1,0:T(8,128)(2,1)S(1)}, u32[]{:S(2)}, u32[]{:S(2)}) collective-permute-start(bf16[192,512]{1,0:T(8,128)(2,1)S(1)} %slice.111), channel_id=1, source_target_pairs={{0,7},{1,0},{2,1},{3,2},{4,3},{5,4},{6,5},{7,6},{8,15},{9,8},{10,9... | collective-permute-start | bytes 589832 | tf_op jit(solution)/shard_map/ppermute | solution.py:61
  180.9 5.1 %collective-permute-done.21 = bf16[192,512]{1,0:T(8,128)(2,1)S(1)} collective-permute-done((bf16[192,512]{1,0:T(8,128)(2,1)S(1)}, bf16[192,512]{1,0:T(8,128)(2,1)S(1)}, u32[]{:S(2)}, u32[]{:S(2)}) %collective-permute-start.21) | collective-permute-done | bytes 196640 | tf_op jit(solution)/shard_map/ppermute | solution.py:61
  187.4 40.7 %all_to_all.15 = bf16[64,16,512]{2,1,0:T(8,128)(2,1)S(1)} all-to-all(bf16[64,16,512]{2,1,0:T(8,128)(2,1)S(1)} %bitcast.43), channel_id=1, replica_groups=mesh['expert'=64,'hidden'=8] {'expert'}, dimensions={0} | all-to-all | bytes 2097152 | tf_op jit(solution)/shard_map/all_to_all | solution.py:58
  228.1 2.3 %fusion.9 = bf16[64,512]{1,0:T(8,128)(2,1)} fusion(f32[64,16,64]{0,2,1:T(8,128)S(1)} %copy-done.2, bf16[64,16,512]{2,1,0:T(8,128)(2,1)S(1)} %all_to_all.15), kind=kOutput, calls=%fused_computation.26 | convolution fusion | flops 402685952 | bytes 1376256 | tf_op jit(solution)/shard_map/est,esd->td/dot_general | solution.py:115
  (68 shorter events, 40.3 us)
Async XLA Ops:
  2.3 29.5 %all-to-all-start = ((bf16[64,8,512]{2,1,0:T(8,128)(2,1)}), bf16[64,8,512]{2,1,0:T(8,128)(2,1)}, u32[]{:S(2)}, u32[]{:S(2)}) async-start(bf16[64,8,512]{2,1,0:T(8,128)(2,1)} %get-tuple-element.15), calls=%async_computation | async-start | bytes 1048576 | tf_op jit(solution)/shard_map/all_to_all | solution.py:58
  19.4 25.2 %copy-start.3 = (f32[64,64]{1,0:T(8,128)S(1)}, f32[64,64]{1,0:T(8,128)}, u32[]{:S(2)}) copy-start(f32[64,64]{1,0:T(8,128)} %get-tuple-element.14) | copy-start | bytes 49156
  31.8 22.9 %collective-permute-start = (bf16[512,512]{1,0:T(8,128)(2,1)}, bf16[512,512]{1,0:T(8,128)(2,1)}, u32[]{:S(2)}, u32[]{:S(2)}) collective-permute-start(bf16[512,512]{1,0:T(8,128)(2,1)} %bitcast.5), channel_id=1, source_target_pairs={{0,1},{1,2},{2,3},{3,4},{4,5},{5,6},{6,7},{7,0},{8,9},{9,10},{10,1... | collective-permute-start | bytes 1572872 | tf_op jit(solution)/shard_map/ppermute | solution.py:61
  35.7 20.9 %collective-permute-start.1 = (bf16[512,512]{1,0:T(8,128)(2,1)}, bf16[512,512]{1,0:T(8,128)(2,1)}, u32[]{:S(2)}, u32[]{:S(2)}) collective-permute-start(bf16[512,512]{1,0:T(8,128)(2,1)} %bitcast.5), channel_id=1, source_target_pairs={{0,7},{1,0},{2,1},{3,2},{4,3},{5,4},{6,5},{7,6},{8,15},{9,8},{10,9... | collective-permute-start | bytes 1572872 | tf_op jit(solution)/shard_map/ppermute | solution.py:61
  44.6 23.8 %all-to-all-start.1 = ((bf16[64,8,512]{2,1,0:T(8,128)(2,1)}), bf16[64,8,512]{2,1,0:T(8,128)(2,1)}, u32[]{:S(2)}, u32[]{:S(2)}) async-start(bf16[64,8,512]{2,1,0:T(8,128)(2,1)} %get-tuple-element.19), calls=%async_computation.1 | async-start | bytes 1048576 | tf_op jit(solution)/shard_map/all_to_all | solution.py:58
  54.7 21.9 %collective-permute-start.2 = (bf16[512,512]{1,0:T(8,128)(2,1)}, bf16[512,512]{1,0:T(8,128)(2,1)}, u32[]{:S(2)}, u32[]{:S(2)}) collective-permute-start(bf16[512,512]{1,0:T(8,128)(2,1)} %collective-permute-done), channel_id=1, source_target_pairs={{0,1},{1,2},{2,3},{3,4},{4,5},{5,6},{6,7},{7,0},{8,9},{9,10},{10,1... | collective-permute-start | bytes 1572872 | tf_op jit(solution)/shard_map/ppermute | solution.py:61
  56.6 21.9 %collective-permute-start.3 = (bf16[512,512]{1,0:T(8,128)(2,1)}, bf16[512,512]{1,0:T(8,128)(2,1)}, u32[]{:S(2)}, u32[]{:S(2)}) collective-permute-start(bf16[512,512]{1,0:T(8,128)(2,1)} %collective-permute-done.1), channel_id=1, source_target_pairs={{0,7},{1,0},{2,1},{3,2},{4,3},{5,4},{6,5},{7,6},{8,15},{9,8},{10,9... | collective-permute-start | bytes 1572872 | tf_op jit(solution)/shard_map/ppermute | solution.py:61
  68.5 16.1 %copy-start.1 = (f32[384,512]{1,0:T(8,128)S(1)}, f32[384,512]{1,0:T(8,128)}, u32[]{:S(2)}) copy-start(f32[384,512]{1,0:T(8,128)} %convolution_add_fusion.7) | copy-start | bytes 2359300
  68.5 17.5 %collective-permute-start.7 = (bf16[512,512]{1,0:T(8,128)(2,1)}, bf16[512,512]{1,0:T(8,128)(2,1)S(1)}, u32[]{:S(2)}, u32[]{:S(2)}) collective-permute-start(bf16[512,512]{1,0:T(8,128)(2,1)} %bitcast.6), channel_id=1, source_target_pairs={{0,1},{1,2},{2,3},{3,4},{4,5},{5,6},{6,7},{7,0},{8,9},{9,10},{10,1... | collective-permute-start | bytes 1572872 | tf_op jit(solution)/shard_map/ppermute | solution.py:61
  70.5 17.4 %collective-permute-start.8 = (bf16[512,512]{1,0:T(8,128)(2,1)}, bf16[512,512]{1,0:T(8,128)(2,1)S(1)}, u32[]{:S(2)}, u32[]{:S(2)}) collective-permute-start(bf16[512,512]{1,0:T(8,128)(2,1)} %bitcast.6), channel_id=1, source_target_pairs={{0,7},{1,0},{2,1},{3,2},{4,3},{5,4},{6,5},{7,6},{8,15},{9,8},{10,9... | collective-permute-start | bytes 1572872 | tf_op jit(solution)/shard_map/ppermute | solution.py:61
  76.6 19.7 %collective-permute-start.4 = (bf16[512,512]{1,0:T(8,128)(2,1)}, bf16[512,512]{1,0:T(8,128)(2,1)S(1)}, u32[]{:S(2)}, u32[]{:S(2)}) collective-permute-start(bf16[512,512]{1,0:T(8,128)(2,1)} %collective-permute-done.2), channel_id=1, source_target_pairs={{0,1},{1,2},{2,3},{3,4},{4,5},{5,6},{6,7},{7,0},{8,9},{9,10},{10,1... | collective-permute-start | bytes 1572872 | tf_op jit(solution)/shard_map/ppermute | solution.py:61
  78.5 19.7 %collective-permute-start.5 = (bf16[512,512]{1,0:T(8,128)(2,1)}, bf16[512,512]{1,0:T(8,128)(2,1)S(1)}, u32[]{:S(2)}, u32[]{:S(2)}) collective-permute-start(bf16[512,512]{1,0:T(8,128)(2,1)} %collective-permute-done.3), channel_id=1, source_target_pairs={{0,7},{1,0},{2,1},{3,2},{4,3},{5,4},{6,5},{7,6},{8,15},{9,8},{10,9... | collective-permute-start | bytes 1572872 | tf_op jit(solution)/shard_map/ppermute | solution.py:61
  86.0 21.5 %collective-permute-start.9 = (bf16[512,512]{1,0:T(8,128)(2,1)S(1)}, bf16[512,512]{1,0:T(8,128)(2,1)S(1)}, u32[]{:S(2)}, u32[]{:S(2)}) collective-permute-start(bf16[512,512]{1,0:T(8,128)(2,1)S(1)} %collective-permute-done.7), channel_id=1, source_target_pairs={{0,1},{1,2},{2,3},{3,4},{4,5},{5,6},{6,7},{7,0},{8,9},{9,10},{10,1... | collective-permute-start | bytes 1572872 | tf_op jit(solution)/shard_map/ppermute | solution.py:61
  88.0 21.5 %collective-permute-start.10 = (bf16[512,512]{1,0:T(8,128)(2,1)S(1)}, bf16[512,512]{1,0:T(8,128)(2,1)S(1)}, u32[]{:S(2)}, u32[]{:S(2)}) collective-permute-start(bf16[512,512]{1,0:T(8,128)(2,1)S(1)} %collective-permute-done.8), channel_id=1, source_target_pairs={{0,7},{1,0},{2,1},{3,2},{4,3},{5,4},{6,5},{7,6},{8,15},{9,8},{10,9... | collective-permute-start | bytes 1572872 | tf_op jit(solution)/shard_map/ppermute | solution.py:61
  96.3 22.5 %collective-permute-start.6 = (bf16[512,512]{1,0:T(8,128)(2,1)S(1)}, bf16[512,512]{1,0:T(8,128)(2,1)S(1)}, u32[]{:S(2)}, u32[]{:S(2)}) collective-permute-start(bf16[512,512]{1,0:T(8,128)(2,1)S(1)} %collective-permute-done.4), channel_id=1, source_target_pairs={{0,1},{1,2},{2,3},{3,4},{4,5},{5,6},{6,7},{7,0},{8,9},{9,10},{10,1... | collective-permute-start | bytes 1572872 | tf_op jit(solution)/shard_map/ppermute | solution.py:61
  107.5 22.5 %collective-permute-start.11 = (bf16[512,512]{1,0:T(8,128)(2,1)S(1)}, bf16[512,512]{1,0:T(8,128)(2,1)S(1)}, u32[]{:S(2)}, u32[]{:S(2)}) collective-permute-start(bf16[512,512]{1,0:T(8,128)(2,1)S(1)} %collective-permute-done.9), channel_id=1, source_target_pairs={{0,1},{1,2},{2,3},{3,4},{4,5},{5,6},{6,7},{7,0},{8,9},{9,10},{10,1... | collective-permute-start | bytes 1572872 | tf_op jit(solution)/shard_map/ppermute | solution.py:61
  109.4 22.5 %collective-permute-start.12 = (bf16[512,512]{1,0:T(8,128)(2,1)S(1)}, bf16[512,512]{1,0:T(8,128)(2,1)S(1)}, u32[]{:S(2)}, u32[]{:S(2)}) collective-permute-start(bf16[512,512]{1,0:T(8,128)(2,1)S(1)} %collective-permute-done.10), channel_id=1, source_target_pairs={{0,7},{1,0},{2,1},{3,2},{4,3},{5,4},{6,5},{7,6},{8,15},{9,8},{10,9... | collective-permute-start | bytes 1572872 | tf_op jit(solution)/shard_map/ppermute | solution.py:61
  130.0 9.7 %collective-permute-start.13 = (bf16[256,512]{1,0:T(8,128)(2,1)S(1)}, bf16[256,512]{1,0:T(8,128)(2,1)S(1)}, u32[]{:S(2)}, u32[]{:S(2)}) collective-permute-start(bf16[256,512]{1,0:T(8,128)(2,1)S(1)} %slice.106), channel_id=1, source_target_pairs={{0,1},{1,2},{2,3},{3,4},{4,5},{5,6},{6,7},{7,0},{8,9},{9,10},{10,1... | collective-permute-start | bytes 786440 | tf_op jit(solution)/shard_map/ppermute | solution.py:61
  132.0 8.6 %collective-permute-start.14 = (bf16[256,512]{1,0:T(8,128)(2,1)S(1)}, bf16[256,512]{1,0:T(8,128)(2,1)S(1)}, u32[]{:S(2)}, u32[]{:S(2)}) collective-permute-start(bf16[256,512]{1,0:T(8,128)(2,1)S(1)} %slice.107), channel_id=1, source_target_pairs={{0,7},{1,0},{2,1},{3,2},{4,3},{5,4},{6,5},{7,6},{8,15},{9,8},{10,9... | collective-permute-start | bytes 786440 | tf_op jit(solution)/shard_map/ppermute | solution.py:61
  141.0 8.0 %copy-start = (bf16[1536,512]{1,0:T(8,128)(2,1)S(1)}, bf16[1536,512]{1,0:T(8,128)(2,1)}, u32[]{:S(2)}) copy-start(bf16[1536,512]{1,0:T(8,128)(2,1)} %fusion.3) | copy-start | bytes 4718596
  141.6 11.3 %collective-permute-start.16 = (bf16[192,1024]{1,0:T(8,128)(2,1)S(1)}, bf16[192,1024]{1,0:T(8,128)(2,1)S(1)}, u32[]{:S(2)}, u32[]{:S(2)}) collective-permute-start(bf16[192,1024]{1,0:T(8,128)(2,1)S(1)} %pad_maximum_fusion), channel_id=1, source_target_pairs={{0,7},{1,0},{2,1},{3,2},{4,3},{5,4},{6,5},{7,6},{8,15},{9,8},{10,9... | collective-permute-start | bytes 1179656 | tf_op jit(solution)/shard_map/ppermute | solution.py:61
  146.9 11.3 %collective-permute-start.15 = (bf16[192,1024]{1,0:T(8,128)(2,1)S(1)}, bf16[192,1024]{1,0:T(8,128)(2,1)S(1)}, u32[]{:S(2)}, u32[]{:S(2)}) collective-permute-start(bf16[192,1024]{1,0:T(8,128)(2,1)S(1)} %pad_maximum_fusion), channel_id=1, source_target_pairs={{0,1},{1,2},{2,3},{3,4},{4,5},{5,6},{6,7},{7,0},{8,9},{9,10},{10,1... | collective-permute-start | bytes 1179656 | tf_op jit(solution)/shard_map/ppermute | solution.py:61
  152.9 10.3 %collective-permute-start.18 = (bf16[192,1024]{1,0:T(8,128)(2,1)S(1)}, bf16[192,1024]{1,0:T(8,128)(2,1)S(1)}, u32[]{:S(2)}, u32[]{:S(2)}) collective-permute-start(bf16[192,1024]{1,0:T(8,128)(2,1)S(1)} %collective-permute-done.16), channel_id=1, source_target_pairs={{0,7},{1,0},{2,1},{3,2},{4,3},{5,4},{6,5},{7,6},{8,15},{9,8},{10,9... | collective-permute-start | bytes 1179656 | tf_op jit(solution)/shard_map/ppermute | solution.py:61
  158.2 10.3 %collective-permute-start.17 = (bf16[192,1024]{1,0:T(8,128)(2,1)S(1)}, bf16[192,1024]{1,0:T(8,128)(2,1)S(1)}, u32[]{:S(2)}, u32[]{:S(2)}) collective-permute-start(bf16[192,1024]{1,0:T(8,128)(2,1)S(1)} %collective-permute-done.15), channel_id=1, source_target_pairs={{0,1},{1,2},{2,3},{3,4},{4,5},{5,6},{6,7},{7,0},{8,9},{9,10},{10,1... | collective-permute-start | bytes 1179656 | tf_op jit(solution)/shard_map/ppermute | solution.py:61
  163.2 10.0 %collective-permute-start.20 = (bf16[192,1024]{1,0:T(8,128)(2,1)S(1)}, bf16[192,1024]{1,0:T(8,128)(2,1)S(1)}, u32[]{:S(2)}, u32[]{:S(2)}) collective-permute-start(bf16[192,1024]{1,0:T(8,128)(2,1)S(1)} %collective-permute-done.18), channel_id=1, source_target_pairs={{0,7},{1,0},{2,1},{3,2},{4,3},{5,4},{6,5},{7,6},{8,15},{9,8},{10,9... | collective-permute-start | bytes 1179656 | tf_op jit(solution)/shard_map/ppermute | solution.py:61
  168.6 9.7 %collective-permute-start.19 = (bf16[192,1024]{1,0:T(8,128)(2,1)S(1)}, bf16[192,1024]{1,0:T(8,128)(2,1)S(1)}, u32[]{:S(2)}, u32[]{:S(2)}) collective-permute-start(bf16[192,1024]{1,0:T(8,128)(2,1)S(1)} %collective-permute-done.17), channel_id=1, source_target_pairs={{0,1},{1,2},{2,3},{3,4},{4,5},{5,6},{6,7},{7,0},{8,9},{9,10},{10,1... | collective-permute-start | bytes 1179656 | tf_op jit(solution)/shard_map/ppermute | solution.py:61
  173.3 7.6 %collective-permute-start.22 = (bf16[192,512]{1,0:T(8,128)(2,1)S(1)}, bf16[192,512]{1,0:T(8,128)(2,1)S(1)}, u32[]{:S(2)}, u32[]{:S(2)}) collective-permute-start(bf16[192,512]{1,0:T(8,128)(2,1)S(1)} %slice.111), channel_id=1, source_target_pairs={{0,7},{1,0},{2,1},{3,2},{4,3},{5,4},{6,5},{7,6},{8,15},{9,8},{10,9... | collective-permute-start | bytes 589832 | tf_op jit(solution)/shard_map/ppermute | solution.py:61
  178.3 7.6 %collective-permute-start.21 = (bf16[192,512]{1,0:T(8,128)(2,1)S(1)}, bf16[192,512]{1,0:T(8,128)(2,1)S(1)}, u32[]{:S(2)}, u32[]{:S(2)}) collective-permute-start(bf16[192,512]{1,0:T(8,128)(2,1)S(1)} %slice.110), channel_id=1, source_target_pairs={{0,1},{1,2},{2,3},{3,4},{4,5},{5,6},{6,7},{7,0},{8,9},{9,10},{10,1... | collective-permute-start | bytes 589832 | tf_op jit(solution)/shard_map/ppermute | solution.py:61
  187.3 40.9 %copy-start.2 = (f32[64,16,64]{0,2,1:T(8,128)S(1)}, f32[64,16,64]{0,2,1:T(8,128)}, u32[]{:S(2)}) copy-start(f32[64,16,64]{0,2,1:T(8,128)} %fusion.15) | copy-start | bytes 786436

commit v4 on v3

--- a/solution.py
+++ b/solution.py
@@ -9,10 +9,9 @@
 F32 = jnp.float32
 
 
-def pack_kernel(ids_ref, tokens_ref, first_ref, rest_ref, slots_ref):
+def pack_kernel(ids_ref, tokens_ref, packed_ref, slots_ref):
     experts, tok_rows = slots_ref.shape
-    lo = first_ref.shape[1]
-    width = tokens_ref.shape[1]
+    capacity, width = packed_ref.shape[1:]
     expert = lax.broadcasted_iota(jnp.int32, (experts, tok_rows), 0)
     chosen = expert == ids_ref[0:1, :]
     for k in range(1, ids_ref.shape[0]):
@@ -23,22 +22,23 @@
     ranks = jnp.dot(jnp.where(chosen, 1.0, 0.0).astype(BF16), earlier, preferred_element_type=F32)
     slots = jnp.where(chosen, ranks, -1.0)
     slots_ref[...] = slots
-    slot = lax.broadcasted_iota(jnp.int32, (experts, lo, tok_rows), 1).astype(F32)
-    spread = jnp.broadcast_to(slots[:, None, :], (experts, lo, tok_rows))
-    for group, packed_ref in enumerate((first_ref, rest_ref)):
-        picks = jnp.where(spread == slot + lo * group, 1.0, 0.0).reshape(experts * lo, tok_rows).astype(BF16)
-        values = jnp.dot(picks, tokens_ref[...], preferred_element_type=F32)
-        packed_ref[...] = values.reshape(experts, lo, width).astype(BF16)
+    slot = lax.broadcasted_iota(jnp.int32, (experts, capacity, tok_rows), 1).astype(F32)
+    spread = jnp.broadcast_to(slots[:, None, :], (experts, capacity, tok_rows))
+    picks = jnp.where(spread == slot, 1.0, 0.0).reshape(experts * capacity, tok_rows).astype(BF16)
+    values = jnp.dot(picks, tokens_ref[...], preferred_element_type=F32)
+    packed_ref[...] = values.reshape(experts, capacity, width).astype(BF16)
 
 
-def pack_rows(ids, tokens, experts, lo):
+def pack_rows(ids, tokens, experts, capacity):
     tok_rows, width = tokens.shape
-    packed = jax.ShapeDtypeStruct((experts, lo, width), BF16)
     return pl.pallas_call(
         pack_kernel,
-        out_shape=(packed, packed, jax.ShapeDtypeStruct((experts, tok_rows), F32)),
+        out_shape=(
+            jax.ShapeDtypeStruct((experts, capacity, width), BF16),
+            jax.ShapeDtypeStruct((experts, tok_rows), F32),
+        ),
         in_specs=[pl.BlockSpec(memory_space=pltpu.VMEM)] * 2,
-        out_specs=[pl.BlockSpec(memory_space=pltpu.VMEM)] * 3,
+        out_specs=[pl.BlockSpec(memory_space=pltpu.VMEM)] * 2,
         name="pack_rows",
     )(ids, tokens)
 
@@ -51,8 +51,7 @@
     units = gate_proj.shape[1]
     top_count = expert_ids.shape[1]
     capacity = 2 * tok_rows * top_count // experts_all
-    lo = capacity // 2
-    rows = experts_all * lo
+    rows = experts_all * capacity // 2
 
     def exchange(values):
         return lax.all_to_all(values, "expert", split_axis=0, concat_axis=0, tiled=True)
@@ -67,27 +66,22 @@
             behind, ahead = fetch(behind, -1), fetch(ahead, 1)
             yield n_hidden - step, behind
             yield step, ahead
-        half = values.shape[0] // 2
-        if group == 0:
-            yield n_hidden // 2, fetch(behind, -1)
-        else:
-            yield n_hidden // 2, jnp.concatenate([fetch(behind[:half], -1), fetch(ahead[half:], 1)], axis=0)
+        yield n_hidden // 2, fetch(behind, -1) if group == 0 else fetch(ahead, 1)
 
-    first, rest, slots = pack_rows(expert_ids.T, tokens, experts_all, lo)
+    packed, slots = pack_rows(expert_ids.T, tokens, experts_all, capacity)
 
     both = jnp.concatenate([gate_proj[0], up_proj[0]], axis=0)
     both = lax.dynamic_slice_in_dim(jnp.concatenate([both, both], axis=1), here * width, n_hidden * width, axis=1)
     down = lax.dynamic_slice_in_dim(
         jnp.concatenate([down_proj[0], down_proj[0]], axis=0), here * units, n_hidden * units, axis=0
     )
-    arrived = exchange(first)
-    arrived, rest, both, down = lax.optimization_barrier((arrived, rest, both, down))
-    arrived = [arrived, exchange(rest)]
+    arrived = exchange(packed).reshape(2 * rows, width)
+    arrived, both, down = lax.optimization_barrier((arrived, both, down))
 
     activation = []
     for group in range(2):
         total = 0.0
-        for ahead, block in around(arrived[group].reshape(rows, width), group):
+        for ahead, block in around(arrived[group * rows : (group + 1) * rows], group):
             weight = both[:, ahead * width : (ahead + 1) * width]
             total = total + jnp.einsum("fd,rd->fr", weight, block, preferred_element_type=F32)
         activation.append((jax.nn.silu(total[:units]) * total[units:]).astype(BF16))
@@ -110,8 +104,7 @@
         total = total + out_sums(behind, n_hidden - step) + out_sums(ahead, step)
     opposite = jnp.concatenate([fetch(behind[:, :rows], -1), fetch(ahead[:, rows:], 1)], axis=1)
     total = (total + out_sums(opposite, across)).astype(BF16)
-    total = total.reshape(2, experts_all, lo, width).transpose(1, 0, 2, 3).reshape(experts_all, capacity, width)
-    returned = exchange(total)
+    returned = exchange(total.reshape(experts_all, capacity, width))
     mixed = jnp.einsum(
         "est,esd->td",
         combine,

time: 232 us -> 231 us (level)
  waiting for transfers between devices: 55.5 us -> 62.5 us
  starting transfers between devices: 100 us -> 93.4 us
  matrix products: 20.1 us -> 15 us
  blocking collectives: 40.7 us -> 45.1 us
    all_to_all x2 -> x1, waiting for transfers between devices: 11.9 us -> 18.7 us  [exchange(): lax.all_to_all(values, 'expert', split_axis=0, concat_axis=0, tiled=True)]
    all_to_all x2 -> x1, starting transfers between devices: 18 us -> 11.9 us  [exchange(): lax.all_to_all(values, 'expert', split_axis=0, concat_axis=0, tiled=True)]
    dot_general x16, matrix products: 13.6 us -> 8.46 us  [on_device(): jnp.einsum('fd,rd->fr', weight, block, preferred_element_type=F32)]
    all_to_all x1, blocking collectives: 40.7 us -> 45.1 us  [exchange(): lax.all_to_all(values, 'expert', split_axis=0, concat_axis=0, tiled=True)]
    ppermute x23 -> x22, starting transfers between devices: 82.3 us -> 81.5 us  [fetch(): lax.ppermute(values, 'hidden', [(i, (i - ahead) % n_hidden) for i in rang...]
    ppermute x23 -> x22, waiting for transfers between devices: 43.7 us -> 43.8 us  [fetch(): lax.ppermute(values, 'hidden', [(i, (i - ahead) % n_hidden) for i in rang...]
  transfers between devices with their start and end apart: 25 -> 23, of which waited for: 14 -> 12; matrix products, arithmetic and copies ran while one was open for 11% -> 9% of each run, Pallas kernels for 0% -> 0%
where the time goes in v4:
time: 231 us; the launch traced here: 230 us
  starting transfers between devices  93.4 us (40%)
  waiting for transfers between devices  62.5 us (27%)
  blocking collectives  45.1 us (20%)
  matrix products  15 us (6%)
  other arithmetic  9.23 us (4%)
  Pallas kernels  2.51 us (1%)
    ppermute x22, starting transfers between devices, fetch(): lax.ppermute(values, 'hidden', [(i, (i - ahead) % n_hidden) for i in rang...  81.5 us
    all_to_all x1, blocking collectives, exchange(): lax.all_to_all(values, 'expert', split_axis=0, concat_axis=0, tiled=True)  45.1 us
    ppermute x22, waiting for transfers between devices, fetch(): lax.ppermute(values, 'hidden', [(i, (i - ahead) % n_hidden) for i in rang...  43.8 us
    all_to_all x1, waiting for transfers between devices, exchange(): lax.all_to_all(values, 'expert', split_axis=0, concat_axis=0, tiled=True)  18.7 us
    all_to_all x1, starting transfers between devices, exchange(): lax.all_to_all(values, 'expert', split_axis=0, concat_axis=0, tiled=True)  11.9 us
    dot_general x16, matrix products, on_device(): jnp.einsum('fd,rd->fr', weight, block, preferred_element_type=F32)  8.46 us
  transfers between devices with their start and end apart: 23, of which 12 were waited for; matrix products, arithmetic and copies ran while one was open for 9% of the time, Pallas kernels for 0%

profile of v4, /device:TPU:1, one launch (start us, length us, event | category | flops | bytes accessed | tf_op | source)
XLA Modules:
  0.0 229.8 jit_solution(13338195242385365990)
XLA Ops:
  0.0 2.5 %pack_rows.1 = (bf16[64,16,512]{2,1,0:T(8,128)(2,1)}, f32[64,64]{1,0:T(8,128)}) custom-call(s32[8,64]{1,0:T(8,128)} %bitcast.38, bf16[64,512]{1,0:T(8,128)(2,1)} %tokens_ref.1), custom_call_target="tpu_custom_call" | custom-call | tf_op jit(solution)/shard_map/pack_rows/pallas_call | solution.py:34
  2.5 11.9 %all-to-all-start = ((bf16[64,16,512]{2,1,0:T(8,128)(2,1)}), bf16[64,16,512]{2,1,0:T(8,128)(2,1)}, u32[]{:S(2)}, u32[]{:S(2)}) async-start(bf16[64,16,512]{2,1,0:T(8,128)(2,1)} %get-tuple-element.13), calls=%async_computation | async-start | bytes 2097152 | tf_op jit(solution)/shard_map/all_to_all | solution.py:57
  15.8 3.9 %fusion.3 = bf16[1536,512]{1,0:T(8,128)(2,1)} fusion(s32[]{:T(128)S(6)} %select_n.17, bf16[1536,512]{1,0:T(8,128)(2,1)S(1)} %bitcast.34), kind=kLoop, calls=%fused_computation.10 | loop fusion | flops 3145728 | bytes 3145732 | tf_op jit(solution)/shard_map/concatenate | solution.py:76
  19.7 4.0 %fusion.1 = bf16[384,4096]{1,0:T(8,128)(2,1)S(1)} fusion(s32[]{:T(128)S(6)} %select_n.16, bf16[192,4096]{1,0:T(8,128)(2,1)} %bitcast.35, bf16[192,4096]{1,0:T(8,128)(2,1)} %bitcast.36), kind=kLoop, calls=%fused_computation.5 | loop fusion | flops 12582912 | bytes 6291460 | tf_op jit(solution)/shard_map/concatenate | solution.py:74
  23.7 18.7 %all-to-all-done = bf16[64,16,512]{2,1,0:T(8,128)(2,1)} async-done(((bf16[64,16,512]{2,1,0:T(8,128)(2,1)}), bf16[64,16,512]{2,1,0:T(8,128)(2,1)}, u32[]{:S(2)}, u32[]{:S(2)}) %all-to-all-start) | async-done | bytes 1048608 | tf_op jit(solution)/shard_map/all_to_all | solution.py:57
  43.7 4.0 %collective-permute-start = (bf16[512,512]{1,0:T(8,128)(2,1)S(1)}, bf16[512,512]{1,0:T(8,128)(2,1)S(1)}, u32[]{:S(2)}, u32[]{:S(2)}) collective-permute-start(bf16[512,512]{1,0:T(8,128)(2,1)S(1)} %get-tuple-element.19), channel_id=1, source_target_pairs={{0,1},{1,2},{2,3},{3,4},{4,5},{5,6},{6,7},{7,0},{8,9},{9,10},{10,1... | collective-permute-start | bytes 1572872 | tf_op jit(solution)/shard_map/ppermute | solution.py:60
  47.6 8.6 %collective-permute-start.1 = (bf16[512,512]{1,0:T(8,128)(2,1)S(1)}, bf16[512,512]{1,0:T(8,128)(2,1)S(1)}, u32[]{:S(2)}, u32[]{:S(2)}) collective-permute-start(bf16[512,512]{1,0:T(8,128)(2,1)S(1)} %get-tuple-element.19), channel_id=1, source_target_pairs={{0,7},{1,0},{2,1},{3,2},{4,3},{5,4},{6,5},{7,6},{8,15},{9,8},{10,9... | collective-permute-start | bytes 1572872 | tf_op jit(solution)/shard_map/ppermute | solution.py:60
  56.3 1.9 collective-permute-start.7
  58.2 4.6 %collective-permute-start.8 = (bf16[512,512]{1,0:T(8,128)(2,1)S(1)}, bf16[512,512]{1,0:T(8,128)(2,1)S(1)}, u32[]{:S(2)}, u32[]{:S(2)}) collective-permute-start(bf16[512,512]{1,0:T(8,128)(2,1)S(1)} %get-tuple-element.20), channel_id=1, source_target_pairs={{0,7},{1,0},{2,1},{3,2},{4,3},{5,4},{6,5},{7,6},{8,15},{9,8},{10,9... | collective-permute-start | bytes 1572872 | tf_op jit(solution)/shard_map/ppermute | solution.py:60
  65.7 1.9 collective-permute-start.2
  67.6 4.6 %collective-permute-start.3 = (bf16[512,512]{1,0:T(8,128)(2,1)S(1)}, bf16[512,512]{1,0:T(8,128)(2,1)S(1)}, u32[]{:S(2)}, u32[]{:S(2)}) collective-permute-start(bf16[512,512]{1,0:T(8,128)(2,1)S(1)} %collective-permute-done.1), channel_id=1, source_target_pairs={{0,7},{1,0},{2,1},{3,2},{4,3},{5,4},{6,5},{7,6},{8,15},{9,8},{10,9... | collective-permute-start | bytes 1572872 | tf_op jit(solution)/shard_map/ppermute | solution.py:60
  72.2 4.2 %collective-permute-done.7 = bf16[512,512]{1,0:T(8,128)(2,1)S(1)} collective-permute-done((bf16[512,512]{1,0:T(8,128)(2,1)S(1)}, bf16[512,512]{1,0:T(8,128)(2,1)S(1)}, u32[]{:S(2)}, u32[]{:S(2)}) %collective-permute-start.7) | collective-permute-done | bytes 524320 | tf_op jit(solution)/shard_map/ppermute | solution.py:60
  79.2 4.6 %collective-permute-start.10 = (bf16[512,512]{1,0:T(8,128)(2,1)S(1)}, bf16[512,512]{1,0:T(8,128)(2,1)S(1)}, u32[]{:S(2)}, u32[]{:S(2)}) collective-permute-start(bf16[512,512]{1,0:T(8,128)(2,1)S(1)} %collective-permute-done.8), channel_id=1, source_target_pairs={{0,7},{1,0},{2,1},{3,2},{4,3},{5,4},{6,5},{7,6},{8,15},{9,8},{10,9... | collective-permute-start | bytes 1572872 | tf_op jit(solution)/shard_map/ppermute | solution.py:60
  84.6 3.1 %collective-permute-done.2 = bf16[512,512]{1,0:T(8,128)(2,1)S(1)} collective-permute-done((bf16[512,512]{1,0:T(8,128)(2,1)S(1)}, bf16[512,512]{1,0:T(8,128)(2,1)S(1)}, u32[]{:S(2)}, u32[]{:S(2)}) %collective-permute-start.2) | collective-permute-done | bytes 524320 | tf_op jit(solution)/shard_map/ppermute | solution.py:60
  89.6 4.6 %collective-permute-start.5 = (bf16[512,512]{1,0:T(8,128)(2,1)S(1)}, bf16[512,512]{1,0:T(8,128)(2,1)S(1)}, u32[]{:S(2)}, u32[]{:S(2)}) collective-permute-start(bf16[512,512]{1,0:T(8,128)(2,1)S(1)} %collective-permute-done.3), channel_id=1, source_target_pairs={{0,7},{1,0},{2,1},{3,2},{4,3},{5,4},{6,5},{7,6},{8,15},{9,8},{10,9... | collective-permute-start | bytes 1572872 | tf_op jit(solution)/shard_map/ppermute | solution.py:60
  94.2 5.6 %collective-permute-done.10 = bf16[512,512]{1,0:T(8,128)(2,1)S(1)} collective-permute-done((bf16[512,512]{1,0:T(8,128)(2,1)S(1)}, bf16[512,512]{1,0:T(8,128)(2,1)S(1)}, u32[]{:S(2)}, u32[]{:S(2)}) %collective-permute-start.10) | collective-permute-done | bytes 524320 | tf_op jit(solution)/shard_map/ppermute | solution.py:60
  99.8 5.3 %collective-permute-start.12 = (bf16[512,512]{1,0:T(8,128)(2,1)S(1)}, bf16[512,512]{1,0:T(8,128)(2,1)S(1)}, u32[]{:S(2)}, u32[]{:S(2)}) collective-permute-start(bf16[512,512]{1,0:T(8,128)(2,1)S(1)} %collective-permute-done.10), channel_id=1, source_target_pairs={{0,7},{1,0},{2,1},{3,2},{4,3},{5,4},{6,5},{7,6},{8,15},{9,8},{10,9... | collective-permute-start | bytes 1572872 | tf_op jit(solution)/shard_map/ppermute | solution.py:60
  105.5 1.9 collective-permute-start.11
  112.5 9.8 %collective-permute-done.12 = bf16[512,512]{1,0:T(8,128)(2,1)S(1)} collective-permute-done((bf16[512,512]{1,0:T(8,128)(2,1)S(1)}, bf16[512,512]{1,0:T(8,128)(2,1)S(1)}, u32[]{:S(2)}, u32[]{:S(2)}) %collective-permute-start.12) | collective-permute-done | bytes 524320 | tf_op jit(solution)/shard_map/ppermute | solution.py:60
  122.3 5.5 %collective-permute-start.13 = (bf16[512,512]{1,0:T(8,128)(2,1)S(1)}, bf16[512,512]{1,0:T(8,128)(2,1)S(1)}, u32[]{:S(2)}, u32[]{:S(2)}) collective-permute-start(bf16[512,512]{1,0:T(8,128)(2,1)S(1)} %collective-permute-done.12), channel_id=1, source_target_pairs={{0,7},{1,0},{2,1},{3,2},{4,3},{5,4},{6,5},{7,6},{8,15},{9,8},{10,9... | collective-permute-start | bytes 1572872 | tf_op jit(solution)/shard_map/ppermute | solution.py:60
  129.0 7.5 %collective-permute-done.13 = bf16[512,512]{1,0:T(8,128)(2,1)S(1)} collective-permute-done((bf16[512,512]{1,0:T(8,128)(2,1)S(1)}, bf16[512,512]{1,0:T(8,128)(2,1)S(1)}, u32[]{:S(2)}, u32[]{:S(2)}) %collective-permute-start.13) | collective-permute-done | bytes 524320 | tf_op jit(solution)/shard_map/ppermute | solution.py:60
  137.6 5.3 %collective-permute-start.15 = (bf16[192,1024]{1,0:T(8,128)(2,1)S(1)}, bf16[192,1024]{1,0:T(8,128)(2,1)S(1)}, u32[]{:S(2)}, u32[]{:S(2)}) collective-permute-start(bf16[192,1024]{1,0:T(8,128)(2,1)S(1)} %pad_maximum_fusion), channel_id=1, source_target_pairs={{0,7},{1,0},{2,1},{3,2},{4,3},{5,4},{6,5},{7,6},{8,15},{9,8},{10,9... | collective-permute-start | bytes 1179656 | tf_op jit(solution)/shard_map/ppermute | solution.py:60
  143.0 1.9 collective-permute-start.14
  145.4 2.8 %collective-permute-done.15 = bf16[192,1024]{1,0:T(8,128)(2,1)S(1)} collective-permute-done((bf16[192,1024]{1,0:T(8,128)(2,1)S(1)}, bf16[192,1024]{1,0:T(8,128)(2,1)S(1)}, u32[]{:S(2)}, u32[]{:S(2)}) %collective-permute-start.15) | collective-permute-done | bytes 393248 | tf_op jit(solution)/shard_map/ppermute | solution.py:60
  148.1 5.3 %collective-permute-start.17 = (bf16[192,1024]{1,0:T(8,128)(2,1)S(1)}, bf16[192,1024]{1,0:T(8,128)(2,1)S(1)}, u32[]{:S(2)}, u32[]{:S(2)}) collective-permute-start(bf16[192,1024]{1,0:T(8,128)(2,1)S(1)} %collective-permute-done.15), channel_id=1, source_target_pairs={{0,7},{1,0},{2,1},{3,2},{4,3},{5,4},{6,5},{7,6},{8,15},{9,8},{10,9... | collective-permute-start | bytes 1179656 | tf_op jit(solution)/shard_map/ppermute | solution.py:60
  153.5 1.9 collective-permute-start.16
  158.1 5.0 %collective-permute-start.19 = (bf16[192,1024]{1,0:T(8,128)(2,1)S(1)}, bf16[192,1024]{1,0:T(8,128)(2,1)S(1)}, u32[]{:S(2)}, u32[]{:S(2)}) collective-permute-start(bf16[192,1024]{1,0:T(8,128)(2,1)S(1)} %collective-permute-done.17), channel_id=1, source_target_pairs={{0,7},{1,0},{2,1},{3,2},{4,3},{5,4},{6,5},{7,6},{8,15},{9,8},{10,9... | collective-permute-start | bytes 1179656 | tf_op jit(solution)/shard_map/ppermute | solution.py:60
  167.9 5.0 %collective-permute-start.21 = (bf16[192,512]{1,0:T(8,128)(2,1)S(1)}, bf16[192,512]{1,0:T(8,128)(2,1)S(1)}, u32[]{:S(2)}, u32[]{:S(2)}) collective-permute-start(bf16[192,512]{1,0:T(8,128)(2,1)S(1)} %slice.109), channel_id=1, source_target_pairs={{0,7},{1,0},{2,1},{3,2},{4,3},{5,4},{6,5},{7,6},{8,15},{9,8},{10,9... | collective-permute-start | bytes 589832 | tf_op jit(solution)/shard_map/ppermute | solution.py:60
  172.9 1.9 collective-permute-start.20
  175.7 5.3 %collective-permute-done.20 = bf16[192,512]{1,0:T(8,128)(2,1)S(1)} collective-permute-done((bf16[192,512]{1,0:T(8,128)(2,1)S(1)}, bf16[192,512]{1,0:T(8,128)(2,1)S(1)}, u32[]{:S(2)}, u32[]{:S(2)}) %collective-permute-start.20) | collective-permute-done | bytes 196640 | tf_op jit(solution)/shard_map/ppermute | solution.py:60
  182.4 45.1 %all_to_all.10 = bf16[64,16,512]{2,1,0:T(8,128)(2,1)S(1)} all-to-all(bf16[64,16,512]{2,1,0:T(8,128)(2,1)S(1)} %bitcast.33), channel_id=1, replica_groups=mesh['expert'=64,'hidden'=8] {'expert'}, dimensions={0} | all-to-all | bytes 2097152 | tf_op jit(solution)/shard_map/all_to_all | solution.py:57
  227.5 2.3 %fusion.8 = bf16[64,512]{1,0:T(8,128)(2,1)} fusion(f32[64,16,64]{0,2,1:T(8,128)S(1)} %copy-done.1, bf16[64,16,512]{2,1,0:T(8,128)(2,1)S(1)} %all_to_all.10), kind=kOutput, calls=%fused_computation.26 | convolution fusion | flops 402685952 | bytes 1376256 | tf_op jit(solution)/shard_map/est,esd->td/dot_general | solution.py:108
  (66 shorter events, 28.6 us)
Async XLA Ops:
  0.0 14.5 %copy-start.4 = (s32[64,8]{0,1:T(8,128)S(1)}, s32[64,8]{0,1:T(8,128)}, u32[]{:S(2)}) copy-start(s32[64,8]{0,1:T(8,128)} %param.7) | copy-start | bytes 6148
  0.0 14.6 %copy-start.5 = (f32[64,8]{0,1:T(8,128)S(1)}, f32[64,8]{0,1:T(8,128)}, u32[]{:S(2)}) copy-start(f32[64,8]{0,1:T(8,128)} %param.8) | copy-start | bytes 6148
  0.0 15.8 %copy-start.2 = (bf16[1,1536,512]{2,1,0:T(8,128)(2,1)S(1)}, bf16[1,1536,512]{2,1,0:T(8,128)(2,1)}, u32[]{:S(2)}) copy-start(bf16[1,1536,512]{2,1,0:T(8,128)(2,1)} %param.11) | copy-start | bytes 4718596
  2.5 12.1 %copy-start.3 = (f32[64,64]{1,0:T(8,128)S(1)}, f32[64,64]{1,0:T(8,128)}, u32[]{:S(2)}) copy-start(f32[64,64]{1,0:T(8,128)} %get-tuple-element.12) | copy-start | bytes 49156
  2.5 39.9 %all-to-all-start = ((bf16[64,16,512]{2,1,0:T(8,128)(2,1)}), bf16[64,16,512]{2,1,0:T(8,128)(2,1)}, u32[]{:S(2)}, u32[]{:S(2)}) async-start(bf16[64,16,512]{2,1,0:T(8,128)(2,1)} %get-tuple-element.13), calls=%async_computation | async-start | bytes 2097152 | tf_op jit(solution)/shard_map/all_to_all | solution.py:57
  43.7 22.0 %collective-permute-start = (bf16[512,512]{1,0:T(8,128)(2,1)S(1)}, bf16[512,512]{1,0:T(8,128)(2,1)S(1)}, u32[]{:S(2)}, u32[]{:S(2)}) collective-permute-start(bf16[512,512]{1,0:T(8,128)(2,1)S(1)} %get-tuple-element.19), channel_id=1, source_target_pairs={{0,1},{1,2},{2,3},{3,4},{4,5},{5,6},{6,7},{7,0},{8,9},{9,10},{10,1... | collective-permute-start | bytes 1572872 | tf_op jit(solution)/shard_map/ppermute | solution.py:60
  47.6 19.9 %collective-permute-start.1 = (bf16[512,512]{1,0:T(8,128)(2,1)S(1)}, bf16[512,512]{1,0:T(8,128)(2,1)S(1)}, u32[]{:S(2)}, u32[]{:S(2)}) collective-permute-start(bf16[512,512]{1,0:T(8,128)(2,1)S(1)} %get-tuple-element.19), channel_id=1, source_target_pairs={{0,7},{1,0},{2,1},{3,2},{4,3},{5,4},{6,5},{7,6},{8,15},{9,8},{10,9... | collective-permute-start | bytes 1572872 | tf_op jit(solution)/shard_map/ppermute | solution.py:60
  56.3 20.2 %collective-permute-start.7 = (bf16[512,512]{1,0:T(8,128)(2,1)S(1)}, bf16[512,512]{1,0:T(8,128)(2,1)S(1)}, u32[]{:S(2)}, u32[]{:S(2)}) collective-permute-start(bf16[512,512]{1,0:T(8,128)(2,1)S(1)} %get-tuple-element.20), channel_id=1, source_target_pairs={{0,1},{1,2},{2,3},{3,4},{4,5},{5,6},{6,7},{7,0},{8,9},{9,10},{10,1... | collective-permute-start | bytes 1572872 | tf_op jit(solution)/shard_map/ppermute | solution.py:60
  58.2 21.0 %collective-permute-start.8 = (bf16[512,512]{1,0:T(8,128)(2,1)S(1)}, bf16[512,512]{1,0:T(8,128)(2,1)S(1)}, u32[]{:S(2)}, u32[]{:S(2)}) collective-permute-start(bf16[512,512]{1,0:T(8,128)(2,1)S(1)} %get-tuple-element.20), channel_id=1, source_target_pairs={{0,7},{1,0},{2,1},{3,2},{4,3},{5,4},{6,5},{7,6},{8,15},{9,8},{10,9... | collective-permute-start | bytes 1572872 | tf_op jit(solution)/shard_map/ppermute | solution.py:60
  65.7 22.0 %collective-permute-start.2 = (bf16[512,512]{1,0:T(8,128)(2,1)S(1)}, bf16[512,512]{1,0:T(8,128)(2,1)S(1)}, u32[]{:S(2)}, u32[]{:S(2)}) collective-permute-start(bf16[512,512]{1,0:T(8,128)(2,1)S(1)} %collective-permute-done), channel_id=1, source_target_pairs={{0,1},{1,2},{2,3},{3,4},{4,5},{5,6},{6,7},{7,0},{8,9},{9,10},{10,1... | collective-permute-start | bytes 1572872 | tf_op jit(solution)/shard_map/ppermute | solution.py:60
  67.6 22.0 %collective-permute-start.3 = (bf16[512,512]{1,0:T(8,128)(2,1)S(1)}, bf16[512,512]{1,0:T(8,128)(2,1)S(1)}, u32[]{:S(2)}, u32[]{:S(2)}) collective-permute-start(bf16[512,512]{1,0:T(8,128)(2,1)S(1)} %collective-permute-done.1), channel_id=1, source_target_pairs={{0,7},{1,0},{2,1},{3,2},{4,3},{5,4},{6,5},{7,6},{8,15},{9,8},{10,9... | collective-permute-start | bytes 1572872 | tf_op jit(solution)/shard_map/ppermute | solution.py:60
  76.4 29.1 %collective-permute-start.9 = (bf16[512,512]{1,0:T(8,128)(2,1)S(1)}, bf16[512,512]{1,0:T(8,128)(2,1)S(1)}, u32[]{:S(2)}, u32[]{:S(2)}) collective-permute-start(bf16[512,512]{1,0:T(8,128)(2,1)S(1)} %collective-permute-done.7), channel_id=1, source_target_pairs={{0,1},{1,2},{2,3},{3,4},{4,5},{5,6},{6,7},{7,0},{8,9},{9,10},{10,1... | collective-permute-start | bytes 1572872 | tf_op jit(solution)/shard_map/ppermute | solution.py:60
  79.2 20.6 %collective-permute-start.10 = (bf16[512,512]{1,0:T(8,128)(2,1)S(1)}, bf16[512,512]{1,0:T(8,128)(2,1)S(1)}, u32[]{:S(2)}, u32[]{:S(2)}) collective-permute-start(bf16[512,512]{1,0:T(8,128)(2,1)S(1)} %collective-permute-done.8), channel_id=1, source_target_pairs={{0,7},{1,0},{2,1},{3,2},{4,3},{5,4},{6,5},{7,6},{8,15},{9,8},{10,9... | collective-permute-start | bytes 1572872 | tf_op jit(solution)/shard_map/ppermute | solution.py:60
  87.7 22.5 %collective-permute-start.4 = (bf16[512,512]{1,0:T(8,128)(2,1)S(1)}, bf16[512,512]{1,0:T(8,128)(2,1)S(1)}, u32[]{:S(2)}, u32[]{:S(2)}) collective-permute-start(bf16[512,512]{1,0:T(8,128)(2,1)S(1)} %collective-permute-done.2), channel_id=1, source_target_pairs={{0,1},{1,2},{2,3},{3,4},{4,5},{5,6},{6,7},{7,0},{8,9},{9,10},{10,1... | collective-permute-start | bytes 1572872 | tf_op jit(solution)/shard_map/ppermute | solution.py:60
  89.6 22.5 %collective-permute-start.5 = (bf16[512,512]{1,0:T(8,128)(2,1)S(1)}, bf16[512,512]{1,0:T(8,128)(2,1)S(1)}, u32[]{:S(2)}, u32[]{:S(2)}) collective-permute-start(bf16[512,512]{1,0:T(8,128)(2,1)S(1)} %collective-permute-done.3), channel_id=1, source_target_pairs={{0,7},{1,0},{2,1},{3,2},{4,3},{5,4},{6,5},{7,6},{8,15},{9,8},{10,9... | collective-permute-start | bytes 1572872 | tf_op jit(solution)/shard_map/ppermute | solution.py:60
  99.8 22.5 %collective-permute-start.12 = (bf16[512,512]{1,0:T(8,128)(2,1)S(1)}, bf16[512,512]{1,0:T(8,128)(2,1)S(1)}, u32[]{:S(2)}, u32[]{:S(2)}) collective-permute-start(bf16[512,512]{1,0:T(8,128)(2,1)S(1)} %collective-permute-done.10), channel_id=1, source_target_pairs={{0,7},{1,0},{2,1},{3,2},{4,3},{5,4},{6,5},{7,6},{8,15},{9,8},{10,9... | collective-permute-start | bytes 1572872 | tf_op jit(solution)/shard_map/ppermute | solution.py:60
  105.5 23.1 %collective-permute-start.11 = (bf16[512,512]{1,0:T(8,128)(2,1)S(1)}, bf16[512,512]{1,0:T(8,128)(2,1)S(1)}, u32[]{:S(2)}, u32[]{:S(2)}) collective-permute-start(bf16[512,512]{1,0:T(8,128)(2,1)S(1)} %collective-permute-done.9), channel_id=1, source_target_pairs={{0,1},{1,2},{2,3},{3,4},{4,5},{5,6},{6,7},{7,0},{8,9},{9,10},{10,1... | collective-permute-start | bytes 1572872 | tf_op jit(solution)/shard_map/ppermute | solution.py:60
  110.1 26.9 %collective-permute-start.6 = (bf16[512,512]{1,0:T(8,128)(2,1)S(1)}, bf16[512,512]{1,0:T(8,128)(2,1)S(1)}, u32[]{:S(2)}, u32[]{:S(2)}) collective-permute-start(bf16[512,512]{1,0:T(8,128)(2,1)S(1)} %collective-permute-done.4), channel_id=1, source_target_pairs={{0,1},{1,2},{2,3},{3,4},{4,5},{5,6},{6,7},{7,0},{8,9},{9,10},{10,1... | collective-permute-start | bytes 1572872 | tf_op jit(solution)/shard_map/ppermute | solution.py:60
  122.3 14.2 %collective-permute-start.13 = (bf16[512,512]{1,0:T(8,128)(2,1)S(1)}, bf16[512,512]{1,0:T(8,128)(2,1)S(1)}, u32[]{:S(2)}, u32[]{:S(2)}) collective-permute-start(bf16[512,512]{1,0:T(8,128)(2,1)S(1)} %collective-permute-done.12), channel_id=1, source_target_pairs={{0,7},{1,0},{2,1},{3,2},{4,3},{5,4},{6,5},{7,6},{8,15},{9,8},{10,9... | collective-permute-start | bytes 1572872 | tf_op jit(solution)/shard_map/ppermute | solution.py:60
  137.0 7.9 %copy-start = (bf16[1536,512]{1,0:T(8,128)(2,1)S(1)}, bf16[1536,512]{1,0:T(8,128)(2,1)}, u32[]{:S(2)}) copy-start(bf16[1536,512]{1,0:T(8,128)(2,1)} %fusion.3) | copy-start | bytes 4718596
  137.6 10.5 %collective-permute-start.15 = (bf16[192,1024]{1,0:T(8,128)(2,1)S(1)}, bf16[192,1024]{1,0:T(8,128)(2,1)S(1)}, u32[]{:S(2)}, u32[]{:S(2)}) collective-permute-start(bf16[192,1024]{1,0:T(8,128)(2,1)S(1)} %pad_maximum_fusion), channel_id=1, source_target_pairs={{0,7},{1,0},{2,1},{3,2},{4,3},{5,4},{6,5},{7,6},{8,15},{9,8},{10,9... | collective-permute-start | bytes 1179656 | tf_op jit(solution)/shard_map/ppermute | solution.py:60
  143.0 10.5 %collective-permute-start.14 = (bf16[192,1024]{1,0:T(8,128)(2,1)S(1)}, bf16[192,1024]{1,0:T(8,128)(2,1)S(1)}, u32[]{:S(2)}, u32[]{:S(2)}) collective-permute-start(bf16[192,1024]{1,0:T(8,128)(2,1)S(1)} %pad_maximum_fusion), channel_id=1, source_target_pairs={{0,1},{1,2},{2,3},{3,4},{4,5},{5,6},{6,7},{7,0},{8,9},{9,10},{10,1... | collective-permute-start | bytes 1179656 | tf_op jit(solution)/shard_map/ppermute | solution.py:60
  148.1 10.0 %collective-permute-start.17 = (bf16[192,1024]{1,0:T(8,128)(2,1)S(1)}, bf16[192,1024]{1,0:T(8,128)(2,1)S(1)}, u32[]{:S(2)}, u32[]{:S(2)}) collective-permute-start(bf16[192,1024]{1,0:T(8,128)(2,1)S(1)} %collective-permute-done.15), channel_id=1, source_target_pairs={{0,7},{1,0},{2,1},{3,2},{4,3},{5,4},{6,5},{7,6},{8,15},{9,8},{10,9... | collective-permute-start | bytes 1179656 | tf_op jit(solution)/shard_map/ppermute | solution.py:60
  153.5 9.7 %collective-permute-start.16 = (bf16[192,1024]{1,0:T(8,128)(2,1)S(1)}, bf16[192,1024]{1,0:T(8,128)(2,1)S(1)}, u32[]{:S(2)}, u32[]{:S(2)}) collective-permute-start(bf16[192,1024]{1,0:T(8,128)(2,1)S(1)} %collective-permute-done.14), channel_id=1, source_target_pairs={{0,1},{1,2},{2,3},{3,4},{4,5},{5,6},{6,7},{7,0},{8,9},{9,10},{10,1... | collective-permute-start | bytes 1179656 | tf_op jit(solution)/shard_map/ppermute | solution.py:60
  158.1 9.7 %collective-permute-start.19 = (bf16[192,1024]{1,0:T(8,128)(2,1)S(1)}, bf16[192,1024]{1,0:T(8,128)(2,1)S(1)}, u32[]{:S(2)}, u32[]{:S(2)}) collective-permute-start(bf16[192,1024]{1,0:T(8,128)(2,1)S(1)} %collective-permute-done.17), channel_id=1, source_target_pairs={{0,7},{1,0},{2,1},{3,2},{4,3},{5,4},{6,5},{7,6},{8,15},{9,8},{10,9... | collective-permute-start | bytes 1179656 | tf_op jit(solution)/shard_map/ppermute | solution.py:60
  163.2 9.7 %collective-permute-start.18 = (bf16[192,1024]{1,0:T(8,128)(2,1)S(1)}, bf16[192,1024]{1,0:T(8,128)(2,1)S(1)}, u32[]{:S(2)}, u32[]{:S(2)}) collective-permute-start(bf16[192,1024]{1,0:T(8,128)(2,1)S(1)} %collective-permute-done.16), channel_id=1, source_target_pairs={{0,1},{1,2},{2,3},{3,4},{4,5},{5,6},{6,7},{7,0},{8,9},{9,10},{10,1... | collective-permute-start | bytes 1179656 | tf_op jit(solution)/shard_map/ppermute | solution.py:60
  167.9 7.8 %collective-permute-start.21 = (bf16[192,512]{1,0:T(8,128)(2,1)S(1)}, bf16[192,512]{1,0:T(8,128)(2,1)S(1)}, u32[]{:S(2)}, u32[]{:S(2)}) collective-permute-start(bf16[192,512]{1,0:T(8,128)(2,1)S(1)} %slice.109), channel_id=1, source_target_pairs={{0,7},{1,0},{2,1},{3,2},{4,3},{5,4},{6,5},{7,6},{8,15},{9,8},{10,9... | collective-permute-start | bytes 589832 | tf_op jit(solution)/shard_map/ppermute | solution.py:60
  172.9 8.1 %collective-permute-start.20 = (bf16[192,512]{1,0:T(8,128)(2,1)S(1)}, bf16[192,512]{1,0:T(8,128)(2,1)S(1)}, u32[]{:S(2)}, u32[]{:S(2)}) collective-permute-start(bf16[192,512]{1,0:T(8,128)(2,1)S(1)} %slice.108), channel_id=1, source_target_pairs={{0,1},{1,2},{2,3},{3,4},{4,5},{5,6},{6,7},{7,0},{8,9},{9,10},{10,1... | collective-permute-start | bytes 589832 | tf_op jit(solution)/shard_map/ppermute | solution.py:60
  182.4 45.1 %copy-start.1 = (f32[64,16,64]{0,2,1:T(8,128)S(1)}, f32[64,16,64]{0,2,1:T(8,128)}, u32[]{:S(2)}) copy-start(f32[64,16,64]{0,2,1:T(8,128)} %fusion.10) | copy-start | bytes 786436
